TPU v7x, 32 devices: a whole 2x2x4 slice. The times are simulated.
32 devices in a mesh: jown: 4 (over y, core), pown: 8 (over z, x).
Axes of the slice: x: 2, y: 2, z: 4, core: 2. Of those that a mesh axis runs over, the one named last changes fastest.
Arguments:
- vertex: bfloat16 [32, 1024, 1024], P(('jown', 'pown')), may hold values from -6 to 6
- bare: bfloat16 [32, 1024, 1024], P(('jown', 'pown')), may hold values from -0.1875 to 0.1875
- pp_prop: float32 [32, 1024], P(('jown', 'pown')), may hold values from 0.3 to 3
- ph_prop: float32 [32, 1024], P(('jown', 'pown')), may hold values from 0.3 to 3
- orders: int32 [32], replicated, may hold values from 512 to 1024, as said below
- pandya_src: int32 [32, 4], replicated, may hold values from 0 to 31
- pandya_sixj: float32 [32, 4, 1024], P(None, None, ('jown', 'pown')), may hold values from -1 to 1
- back_src: int32 [32, 4], replicated, may hold values from 0 to 31
- back_sixj: float32 [32, 4, 1024], P(None, None, ('jown', 'pown')), may hold values from -1 to 1
Outputs:
- updated: bfloat16 [32, 1024, 1024], P(('jown', 'pown'))
Inputs may be any that keep to these rules, and one draw needn't show every extreme that they name: `orders`: some block has order exactly 1024.
All inputs are finite; a program needn't handle non-finite values.
Results may differ from a plain program's by a relative error of at most 0.0055.
Values may be sent and summed in bfloat16 or wider, within the bound.
No kernel may reach another device: no remote copies, remote signals or barrier semaphores. Data moves between devices by JAX's collectives and lax.ppermute only.
A program may use at most 64 MiB of HBM per device.

v0:
```python
import math

import jax
import jax.numpy as jnp
from jax import lax
from jax.sharding import PartitionSpec as P


def recouple(blocks, sources, factors, orders):
    jown_count = lax.axis_size("jown")
    pown_count = lax.axis_size("pown")
    per_owner = blocks.shape[0]
    total = per_owner * jown_count * pown_count
    width = blocks.shape[2]
    positions = jnp.arange(total, dtype=jnp.int32)
    tiles = lax.all_to_all(blocks, ("jown", "pown"), split_axis=1, concat_axis=0, tiled=True)
    tile_rows = tiles.shape[1]
    picks = sources[positions]
    weights = factors[positions]
    live_orders = orders[positions]
    summed = jnp.zeros((total, tile_rows, width), jnp.float32)
    for term in range(picks.shape[1]):
        summed = summed + weights[:, term, :, None] * tiles[picks[:, term]].astype(jnp.float32)
    row_ids = lax.axis_index(("jown", "pown")) * tile_rows + jnp.arange(tile_rows, dtype=jnp.int32)
    col_ids = jnp.arange(width, dtype=jnp.int32)
    keep = (row_ids[None, :, None] < live_orders[:, None, None]) & (
        col_ids[None, None, :] < live_orders[:, None, None]
    )
    mixed = jnp.where(keep, summed, 0.0).astype(jnp.bfloat16)
    return lax.all_to_all(mixed, ("jown", "pown"), split_axis=0, concat_axis=1, tiled=True)


def per_device(
    vertex, bare, pp_prop, ph_prop, orders, pandya_src, pandya_sixj, back_src, back_sixj
):
    per_owner = vertex.shape[0]
    width = vertex.shape[1]
    first = lax.axis_index(("jown", "pown")) * per_owner
    own_orders = lax.dynamic_slice_in_dim(orders, first, per_owner)
    live = (jnp.arange(width, dtype=jnp.int32)[None, :] < own_orders[:, None]).astype(jnp.float32)
    pair_live = live[:, :, None] * live[:, None, :]
    masked = (vertex.astype(jnp.float32) * pair_live).astype(jnp.bfloat16)
    scaled = (pp_prop[:, :, None] * masked.astype(jnp.float32)).astype(jnp.bfloat16)
    ladder = jnp.einsum("bij,bjk->bik", bare, scaled, preferred_element_type=jnp.float32)
    ph_blocks = recouple(masked, pandya_src, pandya_sixj, orders)
    weighted = (ph_blocks.astype(jnp.float32) * ph_prop[:, None, :]).astype(jnp.bfloat16)
    product = jnp.einsum("bij,bjk->bik", weighted, ph_blocks, preferred_element_type=jnp.float32)
    cycle = (product * (1.0 / math.sqrt(width))).astype(jnp.bfloat16)
    returned = recouple(cycle, back_src, back_sixj, orders)
    total = masked.astype(jnp.float32) + ladder + returned.astype(jnp.float32)
    return (total * pair_live).astype(jnp.bfloat16)


def solution(mesh):
    placed = (
        P(("jown", "pown"), None, None),
        P(("jown", "pown"), None, None),
        P(("jown", "pown"), None),
        P(("jown", "pown"), None),
        P(),
        P(),
        P(None, None, ("jown", "pown")),
        P(),
        P(None, None, ("jown", "pown")),
    )
    return jax.shard_map(
        per_device,
        mesh=mesh,
        in_specs=placed,
        out_specs=P(("jown", "pown"), None, None),
        check_vma=False,
    )
```

profile of v0, /device:TPU:0, one launch (start us, length us, event | category | flops | bytes accessed | tf_op | source)
XLA Modules:
  0.0 369.3 jit_solution(16466763152482110455)
XLA Ops:
  0.0 0.0 copy-start
  0.0 1.4 dynamic_slice.3
  1.4 0.6 fusion.19
  2.0 3.9 %copy.27 = bf16[1,1024,1024]{1,2,0:T(8,128)(2,1)} copy(bf16[1,1024,1024]{2,1,0:T(8,128)(2,1)} %param.9) | data formatting | bytes 4194304 | tf_op args[0]
  6.0 3.5 fusion.4
  9.5 10.8 %copy.28 = bf16[1,1024,1024]{2,0,1:T(2,128)(2,1)} copy(bf16[1,1024,1024]{1,2,0:T(8,128)(2,1)} %fusion.4) | data formatting | bytes 4194304 | tf_op jit(solution)/shard_map/convert_element_type | solution.py:42
  20.3 0.6 broadcast.197
  20.9 14.1 %reduce.16 = bf16[1024,1024]{1,0:T(8,128)(2,1)} reduce(bf16[1024,1,1024]{2,1,0:T(2,128)(2,1)} %bitcast.47, bf16[]{:T(256)} %broadcast.197), dimensions={1}, to_apply=%bitcast.30.reduce_sub_computation | reduce | bytes 4194306
  35.0 4.5 %reshape.312 = bf16[32,2,16384]{2,1,0:T(2,128)(2,1)} reshape(bf16[1024,1024]{1,0:T(8,128)(2,1)} %reduce.16) | data formatting | bytes 4194304
  39.5 0.0 copy-start.5
  39.5 0.0 copy-start.1
  39.5 0.0 copy-start.2
  39.5 7.5 %all-to-all-start = ((bf16[32,2,16384]{2,1,0:T(2,128)(2,1)}), bf16[32,2,16384]{2,1,0:T(2,128)(2,1)}, u32[]{:S(2)}, u32[]{:S(2)}) async-start(bf16[32,2,16384]{2,1,0:T(2,128)(2,1)} %reshape.312), calls=%async_computation | async-start | bytes 4194304 | tf_op jit(solution)/shard_map/all_to_all | solution.py:16
  46.9 0.0 copy-done.5
  47.0 0.1 copy.29
  47.1 0.0 copy-done.1
  47.1 0.7 gather_fusion
  47.8 0.6 gather_fusion.3
  48.3 0.0 copy-done.2
  48.4 0.6 gather_fusion.2
  49.0 0.2 fusion.11
  49.2 0.1 broadcast_compare_fusion
  49.3 0.1 iota_compare_fusion
  49.4 47.4 %all-to-all-done = bf16[32,2,16384]{2,1,0:T(2,128)(2,1)} async-done(((bf16[32,2,16384]{2,1,0:T(2,128)(2,1)}), bf16[32,2,16384]{2,1,0:T(2,128)(2,1)}, u32[]{:S(2)}, u32[]{:S(2)}) %all-to-all-start) | async-done | bytes 2097184 | tf_op jit(solution)/shard_map/all_to_all | solution.py:16
  96.9 10.5 %reshape.313 = bf16[1024,1,1024]{2,1,0:T(2,128)(2,1)} reshape(bf16[32,2,16384]{2,1,0:T(2,128)(2,1)} %all-to-all-done) | data formatting | bytes 4194304
  107.3 4.3 %copy.34 = bf16[1,1024,1024]{2,1,0:T(8,128)(2,1)} copy(bf16[1,1024,1024]{2,0,1:T(2,128)(2,1)} %bitcast.49) | data formatting | bytes 4194304
  111.6 3.7 gather_fusion.4
  115.3 3.6 gather_fusion.5
  118.9 3.6 gather_fusion.6
  122.5 3.6 gather_fusion.7
  126.1 4.5 %fusion.2 = bf16[32,32,1024]{2,1,0:T(8,128)(2,1)S(1)} fusion(bf16[32,32,1024]{2,1,0:T(8,128)(2,1)} %gather_fusion.7, bf16[32,32,1024]{2,1,0:T(8,128)(2,1)} %gather_fusion.6, bf16[32,32,1024]{2,1,0:T(8,128)(2,1)} %gather_fusion.5, bf16[32,32,1024]{2,1,0:T(8,128)(2,1)} %gather_fusion.4, f32[32,32]{1,0:T(8,128)S(1)} %bitcast.61, f32[32,32]{1,0:T(8,128)S(1)} %bitcast.59, ...), kind=kLoop, calls=%fused_computation.21 | loop fusion | flops 14680064 | bytes 10535936 | tf_op jit(solution)/shard_map/convert_element_type | solution.py:29
  130.6 0.0 copy-start.4
  130.6 52.7 %all_to_all.45 = bf16[32,32,1024]{2,1,0:T(8,128)(2,1)S(1)} all-to-all(bf16[32,32,1024]{2,1,0:T(8,128)(2,1)S(1)} %fusion.2), channel_id=1, replica_groups=mesh['jown'=4,'pown'=8] {'jown','pown'}, dimensions={0} | all-to-all | bytes 4194304 | tf_op jit(solution)/shard_map/all_to_all | solution.py:30
  183.4 0.0 copy-done.4
  183.4 0.6 multiply_convert_fusion.1
  184.0 2.3 fusion.10
  186.3 5.2 %copy.37 = bf16[1,1024,1024]{2,0,1:T(2,128)(2,1)} copy(bf16[1,1024,1024]{2,1,0:T(8,128)(2,1)S(1)} %fusion.10) | data formatting | bytes 4194304 | tf_op jit(solution)/shard_map/convert_element_type | solution.py:48
  191.5 14.1 %reduce.17 = bf16[1024,1024]{1,0:T(8,128)(2,1)} reduce(bf16[1024,1,1024]{2,1,0:T(2,128)(2,1)} %bitcast.48, bf16[]{:T(256)} %broadcast.197), dimensions={1}, to_apply=%bitcast.37.reduce_sub_computation | reduce | bytes 4194306
  205.6 4.5 %reshape.314 = bf16[32,2,16384]{2,1,0:T(2,128)(2,1)} reshape(bf16[1024,1024]{1,0:T(8,128)(2,1)} %reduce.17) | data formatting | bytes 4194304
  210.1 0.0 copy-start.6
  210.1 0.0 copy-start.3
  210.1 3.6 all-to-all-start.2
  213.8 0.0 copy-done.6
  213.8 0.1 copy.31
  213.9 0.6 gather_fusion.8
  214.4 0.0 copy-done.3
  214.4 0.6 gather_fusion.1
  215.0 0.2 fusion.15
  215.3 48.3 %all-to-all-done.2 = bf16[32,2,16384]{2,1,0:T(2,128)(2,1)} async-done(((bf16[32,2,16384]{2,1,0:T(2,128)(2,1)}), bf16[32,2,16384]{2,1,0:T(2,128)(2,1)}, u32[]{:S(2)}, u32[]{:S(2)}) %all-to-all-start.2) | async-done | bytes 2097184 | tf_op jit(solution)/shard_map/all_to_all | solution.py:16
  263.7 10.5 %reshape.315 = bf16[1024,1,1024]{2,1,0:T(2,128)(2,1)} reshape(bf16[32,2,16384]{2,1,0:T(2,128)(2,1)} %all-to-all-done.2) | data formatting | bytes 4194304
  274.1 4.3 %copy.35 = bf16[1,1024,1024]{2,1,0:T(8,128)(2,1)} copy(bf16[1,1024,1024]{2,0,1:T(2,128)(2,1)} %bitcast.50) | data formatting | bytes 4194304
  278.5 3.6 gather_fusion.10
  282.1 3.6 gather_fusion.11
  285.6 3.7 gather_fusion.9
  289.3 3.6 gather_fusion.12
  292.9 4.5 %fusion.3 = bf16[32,32,1024]{2,1,0:T(8,128)(2,1)S(1)} fusion(bf16[32,32,1024]{2,1,0:T(8,128)(2,1)} %gather_fusion.12, bf16[32,32,1024]{2,1,0:T(8,128)(2,1)} %gather_fusion.11, bf16[32,32,1024]{2,1,0:T(8,128)(2,1)} %gather_fusion.10, bf16[32,32,1024]{2,1,0:T(8,128)(2,1)} %gather_fusion.9, f32[32,32]{1,0:T(8,128)S(1)} %bitcast.57, f32[32,32]{1,0:T(8,128)S(1)} %bitcast.55, ...), kind=kLoop, calls=%fused_computation.22 | loop fusion | flops 14680064 | bytes 10535936 | tf_op jit(solution)/shard_map/convert_element_type | solution.py:29
  297.4 52.7 %all_to_all.46 = bf16[32,32,1024]{2,1,0:T(8,128)(2,1)S(1)} all-to-all(bf16[32,32,1024]{2,1,0:T(8,128)(2,1)S(1)} %fusion.3), channel_id=1, replica_groups=mesh['jown'=4,'pown'=8] {'jown','pown'}, dimensions={0} | all-to-all | bytes 4194304 | tf_op jit(solution)/shard_map/all_to_all | solution.py:30
  350.1 2.4 bitcast_convert_fusion
  352.5 0.0 copy-start.7
  352.5 5.4 %copy.32 = f32[1,1024,1024]{1,2,0:T(8,128)} copy(f32[1,1024,1024]{2,1,0:T(8,128)} %bitcast_convert_fusion) | data formatting | bytes 8388608 | tf_op jit(solution)/shard_map/convert_element_type | solution.py:50
  357.9 0.0 copy-done
  357.9 0.0 copy-done.7
  357.9 7.4 %fusion.5 = bf16[1,1024,1024]{1,2,0:T(8,128)(2,1)} fusion(f32[1,1024,1024]{1,2,0:T(8,128)} %copy.32, bf16[1,1024,1024]{2,1,0:T(8,128)(2,1)S(1)} %copy-done, f32[1024]{0:T(1024)S(1)} %bitcast.63, f32[1024]{0:T(1024)S(1)} %fusion.19, bf16[1,1024,1024]{1,2,0:T(8,128)(2,1)} %copy.27), kind=kOutput, calls=%fused_computation.24 | convolution fusion | flops 2164260864 | bytes 10493952 | tf_op jit(solution)/shard_map/bij,bjk->bik/dot_general | solution.py:44
  365.3 3.9 %copy.33 = bf16[1,1024,1024]{2,1,0:T(8,128)(2,1)} copy(bf16[1,1024,1024]{1,2,0:T(8,128)(2,1)} %fusion.5) | data formatting | bytes 4194304 | tf_op jit(solution)/shard_map/convert_element_type | solution.py:51
  (9 shorter events, 0.1 us)
Async XLA Ops:
  0.0 357.9 %copy-start = (bf16[1,1024,1024]{2,1,0:T(8,128)(2,1)S(1)}, bf16[1,1024,1024]{2,1,0:T(8,128)(2,1)}, u32[]{:S(2)}) copy-start(bf16[1,1024,1024]{2,1,0:T(8,128)(2,1)} %param.10) | copy-start | bytes 6291460
  39.5 7.5 %copy-start.5 = (s32[32,4]{0,1:T(4,128)S(1)}, s32[32,4]{0,1:T(4,128)}, u32[]{:S(2)}) copy-start(s32[32,4]{0,1:T(4,128)} %param.14) | copy-start | bytes 1540
  39.5 7.6 %copy-start.1 = (s32[32]{0:T(128)S(1)}, s32[32]{0:T(128)}, u32[]{:S(2)}) copy-start(s32[32]{0:T(128)} %param.13) | copy-start | bytes 388
  39.5 8.9 %copy-start.2 = (f32[32,4,32]{2,1,0:T(4,128)S(1)}, f32[32,4,32]{2,1,0:T(4,128)}, u32[]{:S(2)}) copy-start(f32[32,4,32]{2,1,0:T(4,128)} %param.15) | copy-start | bytes 49156
  39.5 57.4 %all-to-all-start = ((bf16[32,2,16384]{2,1,0:T(2,128)(2,1)}), bf16[32,2,16384]{2,1,0:T(2,128)(2,1)}, u32[]{:S(2)}, u32[]{:S(2)}) async-start(bf16[32,2,16384]{2,1,0:T(2,128)(2,1)} %reshape.312), calls=%async_computation | async-start | bytes 4194304 | tf_op jit(solution)/shard_map/all_to_all | solution.py:16
  130.6 52.7 %copy-start.4 = (f32[1,1024]{1,0:T(1,128)S(1)}, f32[1,1024]{1,0:T(1,128)}, u32[]{:S(2)}) copy-start(f32[1,1024]{1,0:T(1,128)} %param.12) | copy-start | bytes 12292
  210.1 3.6 copy-start.6
  210.1 4.3 %copy-start.3 = (f32[32,4,32]{2,1,0:T(4,128)S(1)}, f32[32,4,32]{2,1,0:T(4,128)}, u32[]{:S(2)}) copy-start(f32[32,4,32]{2,1,0:T(4,128)} %param.17) | copy-start | bytes 49156
  210.1 53.5 %all-to-all-start.2 = ((bf16[32,2,16384]{2,1,0:T(2,128)(2,1)}), bf16[32,2,16384]{2,1,0:T(2,128)(2,1)}, u32[]{:S(2)}, u32[]{:S(2)}) async-start(bf16[32,2,16384]{2,1,0:T(2,128)(2,1)} %reshape.314), calls=%async_computation.2 | async-start | bytes 4194304 | tf_op jit(solution)/shard_map/all_to_all | solution.py:16
  352.5 5.4 %copy-start.7 = (f32[1,1024]{1,0:T(1,128)S(1)}, f32[1,1024]{1,0:T(1,128)}, u32[]{:S(2)}) copy-start(f32[1,1024]{1,0:T(1,128)} %param.11) | copy-start | bytes 12292
where the time goes:
time: 371 us; the launch traced here: 369 us
  blocking collectives  105 us (28%)
  local copies, waits for them, and re-layouts  102 us (27%)
  waiting for transfers between devices  95.7 us (26%)
  other arithmetic  45.1 us (12%)
  starting transfers between devices  11.1 us (3%)
  matrix products  9.76 us (3%)
    all_to_all x2, blocking collectives, recouple(): lax.all_to_all(mixed, ('jown', 'pown'), split_axis=0, concat_axis=1, tile...  105 us
    all_to_all x2, waiting for transfers between devices, recouple(): lax.all_to_all(blocks, ('jown', 'pown'), split_axis=1, concat_axis=0, til...  95.7 us
    unnamed x26, local copies, waits for them, and re-layouts  43.3 us
    gather x8, local copies, waits for them, and re-layouts, recouple(): tiles[picks[:, term]].astype(jnp.float32)  28.9 us
    unnamed x2, other arithmetic  28.3 us
    all_to_all x2, starting transfers between devices, recouple(): lax.all_to_all(blocks, ('jown', 'pown'), split_axis=1, concat_axis=0, til...  11.1 us
    convert_element_type x1, local copies, waits for them, and re-layouts, per_device(): masked = (vertex.astype(jnp.float32) * pair_live).astype(jnp.bfloat16)  10.8 us
    convert_element_type x2, other arithmetic, recouple(): mixed = jnp.where(keep, summed, 0.0).astype(jnp.bfloat16)  9.04 us
  transfers between devices with their start and end apart: 2, of which 2 were waited for; matrix products, arithmetic and copies ran while one was open for 1% of the time, Pallas kernels for 0%

commit v1 on v0

v1 whole, which is shorter than its diff:
```python
import math

import jax
import jax.numpy as jnp
from jax import lax
from jax.experimental import pallas as pl
from jax.experimental.pallas import tpu as pltpu
from jax.sharding import PartitionSpec as P

AXES = ("jown", "pown")


def recouple_body(src, orders, first, factors, tiles, mixed):
    total, rows, width = tiles.shape
    terms = src.shape[1]
    row_ids = first[0] + lax.broadcasted_iota(jnp.int32, (rows, 1), 0)
    col_ids = lax.broadcasted_iota(jnp.int32, (1, width), 1)

    def one(c, carry):
        own = orders[c]
        weights = factors[c]
        summed = jnp.zeros((rows, width), jnp.float32)
        for k in range(terms):
            pick = src[c, k]
            live = jnp.minimum(own, orders[pick])
            weight = jnp.where(row_ids < live, weights[:, k : k + 1], 0.0)
            part = weight * tiles[pick].astype(jnp.float32)
            summed = summed + jnp.where(col_ids < live, part, 0.0)
        mixed[c] = summed.astype(jnp.bfloat16)
        return carry

    lax.fori_loop(0, total, one, 0)


def recouple_tiles(tiles, src, factors, orders):
    total, rows, width = tiles.shape
    first = (lax.axis_index(AXES) * rows).reshape(1)
    smem = pl.BlockSpec(memory_space=pltpu.SMEM)
    vmem = pl.BlockSpec(memory_space=pltpu.VMEM)
    return pl.pallas_call(
        recouple_body,
        out_shape=jax.ShapeDtypeStruct((total, rows, width), jnp.bfloat16),
        in_specs=[smem, smem, smem, vmem, vmem],
        out_specs=vmem,
        cost_estimate=pl.CostEstimate(
            flops=8 * total * rows * width,
            bytes_accessed=4 * total * rows * width,
            transcendentals=0,
        ),
    )(src, orders, first, jnp.swapaxes(factors, 1, 2), tiles)


def ladder_body(order, bare, vertex, prop, base, scaled):
    rows, width = base.shape
    step = pl.program_id(0)
    own = order[0]
    row_ids = lax.broadcasted_iota(jnp.int32, (width, 1), 0)
    col_ids = lax.broadcasted_iota(jnp.int32, (1, width), 1)

    @pl.when(step == 0)
    def _():
        def fill(i, carry):
            at = pl.ds(pl.multiple_of(i * rows, rows), rows)
            ids = i * rows + lax.broadcasted_iota(jnp.int32, (rows, 1), 0)
            weight = jnp.where(ids < own, prop[at, :], 0.0)
            part = weight * vertex[at, :].astype(jnp.float32)
            scaled[at, :] = jnp.where(col_ids < own, part, 0.0).astype(jnp.bfloat16)
            return carry

        lax.fori_loop(0, width // rows, fill, 0)

    at = pl.ds(pl.multiple_of(step * rows, rows), rows)
    product = jnp.dot(bare[...], scaled[...], preferred_element_type=jnp.float32)
    total = vertex[at, :].astype(jnp.float32) + product
    live = (step * rows + row_ids[:rows] < own) & (col_ids < own)
    base[...] = jnp.where(live, total, 0.0)


def ladder_base(order, bare, vertex, prop):
    width = vertex.shape[0]
    rows = min(256, width)
    whole = pl.BlockSpec((width, width), lambda i: (0, 0))
    return pl.pallas_call(
        ladder_body,
        grid=(width // rows,),
        out_shape=jax.ShapeDtypeStruct((width, width), jnp.float32),
        in_specs=[
            pl.BlockSpec(memory_space=pltpu.SMEM),
            pl.BlockSpec((rows, width), lambda i: (i, 0)),
            whole,
            pl.BlockSpec((width, 1), lambda i: (0, 0)),
        ],
        out_specs=pl.BlockSpec((rows, width), lambda i: (i, 0)),
        scratch_shapes=[pltpu.VMEM((width, width), jnp.bfloat16)],
        cost_estimate=pl.CostEstimate(
            flops=2 * width**3, bytes_accessed=8 * width * width, transcendentals=0
        ),
    )(order, bare, vertex, prop)


def exchange(tiles):
    return lax.all_to_all(tiles, AXES, split_axis=0, concat_axis=0, tiled=True)


def per_device(
    vertex, bare, pp_prop, ph_prop, orders, pandya_src, pandya_sixj, back_src, back_sixj
):
    per_owner, width, _ = vertex.shape
    parts = lax.axis_size(AXES)
    tile_rows = width // parts
    assert per_owner == 1
    own_order = lax.dynamic_slice_in_dim(orders, lax.axis_index(AXES), 1)

    def to_tiles(block):
        return block.reshape(parts, tile_rows, width)

    def to_block(tiles):
        return tiles.reshape(width, width)

    tiles = exchange(to_tiles(vertex[0]))
    ph = to_block(exchange(recouple_tiles(tiles, pandya_src, pandya_sixj, orders)))
    weighted = (ph.astype(jnp.float32) * ph_prop).astype(jnp.bfloat16)
    product = jnp.dot(weighted, ph, preferred_element_type=jnp.float32)
    cycle = (product * (1.0 / math.sqrt(width))).astype(jnp.bfloat16)
    tiles = exchange(to_tiles(cycle))
    returned = to_block(exchange(recouple_tiles(tiles, back_src, back_sixj, orders)))
    base = ladder_base(own_order, bare[0], vertex[0], pp_prop.reshape(width, 1))
    return (base + returned.astype(jnp.float32)).astype(jnp.bfloat16)[None]


def solution(mesh):
    placed = (
        P(AXES, None, None),
        P(AXES, None, None),
        P(AXES, None),
        P(AXES, None),
        P(),
        P(),
        P(None, None, AXES),
        P(),
        P(None, None, AXES),
    )
    return jax.shard_map(
        per_device,
        mesh=mesh,
        in_specs=placed,
        out_specs=P(AXES, None, None),
        check_vma=False,
    )
```

time: 371 us -> 244 us (0.66)
  local copies, waits for them, and re-layouts: 102 us -> 7.76 us
  blocking collectives: 105 us -> 52.9 us
  waiting for transfers between devices: 95.7 us -> 137 us
  other arithmetic: 45.1 us -> 4.9 us
  Pallas kernels: 0 us -> 24.4 us
  matrix products: 9.76 us -> 3.67 us
    all_to_all x2 -> x1, blocking collectives: 105 us -> 52.9 us  [exchange(): return lax.all_to_all(tiles, AXES, split_axis=0, concat_axis=0, tiled=True)]
    all_to_all x2 -> x3, waiting for transfers between devices: 95.7 us -> 137 us  [exchange(): return lax.all_to_all(tiles, AXES, split_axis=0, concat_axis=0, tiled=True)]
    unnamed x26 -> x22, local copies, waits for them, and re-layouts: 43.3 us -> 6.16 us
    gather x13 -> x0, local copies, waits for them, and re-layouts: 32 us -> none  [the longest x8 28.9 us: recouple(): tiles[picks[:, term]].astype(jnp.float32)]
    unnamed x2 -> x0, other arithmetic: 28.3 us -> none
    convert_element_type x4 -> x0, local copies, waits for them, and re-layouts: 25.3 us -> none  [the longest x1 10.8 us: per_device(): masked = (vertex.astype(jnp.float32) * pair_live).astype(jnp.bfloat16)]
    pallas_call x0 -> x3, Pallas kernels: none -> 24.4 us  [the longest x2 16.5 us: recouple_tiles(): pl.pallas_call(recouple_body, out_shape=jax.ShapeDtypeStruct((total, rows...]
    convert_element_type x6 -> x1, other arithmetic: 16.2 us -> 0.62 us  [per_device(): weighted = (ph.astype(jnp.float32) * ph_prop).astype(jnp.bfloat16)]
  transfers between devices with their start and end apart: 2 -> 3, of which waited for: 2 -> 3; matrix products, arithmetic and copies ran while one was open for 1% -> 2% of each run, Pallas kernels for 0% -> 3%
where the time goes in v1:
time: 244 us
  waiting for transfers between devices  137 us (56%)
  blocking collectives  52.9 us (22%)
  Pallas kernels  24.4 us (10%)
  starting transfers between devices  13.1 us (5%)
  local copies, waits for them, and re-layouts  7.76 us (3%)
  other arithmetic  4.9 us (2%)
  matrix products  3.67 us (2%)
    all_to_all x3, waiting for transfers between devices, exchange(): return lax.all_to_all(tiles, AXES, split_axis=0, concat_axis=0, tiled=True)  137 us
    all_to_all x1, blocking collectives, exchange(): return lax.all_to_all(tiles, AXES, split_axis=0, concat_axis=0, tiled=True)  52.9 us
    pallas_call x2, Pallas kernels, recouple_tiles(): pl.pallas_call(recouple_body, out_shape=jax.ShapeDtypeStruct((total, rows...  16.5 us
    all_to_all x3, starting transfers between devices, exchange(): return lax.all_to_all(tiles, AXES, split_axis=0, concat_axis=0, tiled=True)  13.1 us
    pallas_call x1, Pallas kernels, ladder_base(): pl.pallas_call(ladder_body, grid=(width // rows,), out_shape=jax.ShapeDty...  7.88 us
    unnamed x22, local copies, waits for them, and re-layouts  6.16 us
  transfers between devices with their start and end apart: 3, of which 3 were waited for; matrix products, arithmetic and copies ran while one was open for 2% of the time, Pallas kernels for 3%

profile of v1, /device:TPU:0, one launch (start us, length us, event | category | flops | bytes accessed | tf_op | source)
XLA Modules:
  0.0 243.6 jit_solution(2549528809649227014)
XLA Ops:
  0.0 0.0 copy-start.6
  0.0 0.0 copy-start.2
  0.0 7.3 %all-to-all-start = ((bf16[32,32,1024]{2,1,0:T(8,128)(2,1)}), bf16[32,32,1024]{2,1,0:T(8,128)(2,1)S(1)}, u32[]{:S(2)}, u32[]{:S(2)}) async-start(bf16[32,32,1024]{2,1,0:T(8,128)(2,1)} %bitcast.18), calls=%async_computation | async-start | bytes 4194304 | tf_op jit(solution)/shard_map/all_to_all | solution.py:102
  7.3 0.0 copy-done.6
  7.4 0.7 copy.17.src
  8.0 0.0 copy-done.2
  8.0 1.1 copy.16
  9.1 48.2 %all-to-all-done.tiles = bf16[32,32,1024]{2,1,0:T(8,128)(2,1)S(1)} async-done(((bf16[32,32,1024]{2,1,0:T(8,128)(2,1)}), bf16[32,32,1024]{2,1,0:T(8,128)(2,1)S(1)}, u32[]{:S(2)}, u32[]{:S(2)}) %all-to-all-start) | async-done | bytes 2097184 | tf_op jit(solution)/shard_map/all_to_all | solution.py:102
  57.3 0.0 copy-start
  57.3 1.3 copy-done
  58.6 8.2 %shard_map.92 = bf16[32,32,1024]{2,1,0:T(8,128)(2,1)} custom-call(s32[32,4]{1,0:T(8,128)} %copy.17.src, s32[32]{0:T(128)} %orders.3, s32[1]{0:T(128)} %bitcast.3.first, f32[32,32,4]{2,1,0:T(8,128)} %bitcast.24, bf16[32,32,1024]{2,1,0:T(8,128)(2,1)} %copy-done), custom_call_target="tpu_custom_call" | custom-call | flops 8388608 | bytes 4194304 | tf_op jit(solution)/shard_map/pallas_call | solution.py:40
  66.8 0.0 copy-start.4
  66.8 52.9 %all_to_all.20 = bf16[32,32,1024]{2,1,0:T(8,128)(2,1)S(1)} all-to-all(bf16[32,32,1024]{2,1,0:T(8,128)(2,1)} %shard_map.92), channel_id=1, replica_groups=mesh['jown'=4,'pown'=8] {'jown','pown'}, dimensions={0} | all-to-all | bytes 4194304 | tf_op jit(solution)/shard_map/all_to_all | solution.py:102
  119.8 0.0 copy-done.4
  119.8 0.6 multiply_convert_fusion.1
  120.4 3.7 %multiply_convert_fusion = bf16[1024,1024]{1,0:T(8,128)(2,1)} fusion(bf16[1024,1024]{1,0:T(8,128)(2,1)S(1)} %bitcast.22, bf16[1024,1024]{1,0:T(8,128)(2,1)S(1)} %bitcast.20), kind=kOutput, calls=%fused_computation.2 | convolution fusion | flops 2149580800 | bytes 6291456 | tf_op jit(solution)/shard_map/dot_general | solution.py:123
  124.1 0.0 copy-start.7
  124.1 0.0 copy-start.3
  124.1 2.9 %all-to-all-start.2 = ((bf16[32,32,1024]{2,1,0:T(8,128)(2,1)}), bf16[32,32,1024]{2,1,0:T(8,128)(2,1)S(1)}, u32[]{:S(2)}, u32[]{:S(2)}) async-start(bf16[32,32,1024]{2,1,0:T(8,128)(2,1)} %bitcast.23), calls=%async_computation.2 | async-start | bytes 4194304 | tf_op jit(solution)/shard_map/all_to_all | solution.py:102
  126.9 0.0 copy-done.7
  126.9 0.7 copy.18.src
  127.6 0.0 copy-done.3
  127.6 1.1 copy.15
  128.7 48.2 %all-to-all-done.2.tiles = bf16[32,32,1024]{2,1,0:T(8,128)(2,1)S(1)} async-done(((bf16[32,32,1024]{2,1,0:T(8,128)(2,1)}), bf16[32,32,1024]{2,1,0:T(8,128)(2,1)S(1)}, u32[]{:S(2)}, u32[]{:S(2)}) %all-to-all-start.2) | async-done | bytes 2097184 | tf_op jit(solution)/shard_map/all_to_all | solution.py:102
  176.9 0.0 copy-start.1
  176.9 1.3 copy-done.1
  178.2 8.2 %shard_map.93 = bf16[32,32,1024]{2,1,0:T(8,128)(2,1)} custom-call(s32[32,4]{1,0:T(8,128)} %copy.18.src, s32[32]{0:T(128)} %orders.3, s32[1]{0:T(128)} %bitcast.3.first, f32[32,32,4]{2,1,0:T(8,128)} %bitcast.25, bf16[32,32,1024]{2,1,0:T(8,128)(2,1)} %copy-done.1), custom_call_target="tpu_custom_call" | custom-call | flops 8388608 | bytes 4194304 | tf_op jit(solution)/shard_map/pallas_call | solution.py:40
  186.4 0.0 copy-start.8
  186.4 0.0 copy-start.5
  186.4 2.9 %all-to-all-start.3 = ((bf16[32,32,1024]{2,1,0:T(8,128)(2,1)}), bf16[32,32,1024]{2,1,0:T(8,128)(2,1)S(1)}, u32[]{:S(2)}, u32[]{:S(2)}) async-start(bf16[32,32,1024]{2,1,0:T(8,128)(2,1)} %shard_map.93), calls=%async_computation.3 | async-start | bytes 4194304 | tf_op jit(solution)/shard_map/all_to_all | solution.py:102
  189.4 0.0 copy-done.8
  189.4 0.6 dynamic_slice.3.order
  190.0 0.0 copy-done.5
  190.0 1.0 copy.14.prop
  191.0 7.9 %shard_map.91 = f32[1024,1024]{1,0:T(8,128)} custom-call(s32[1]{0:T(128)} %dynamic_slice.3.order, bf16[1024,1024]{1,0:T(8,128)(2,1)} %bitcast.21, bf16[1024,1024]{1,0:T(8,128)(2,1)} %bitcast.19, f32[1024,1]{1,0:T(8,128)} %copy.14.prop), custom_call_target="tpu_custom_call" | custom-call | flops 2147483648 | bytes 8388608 | tf_op jit(solution)/shard_map/pallas_call | solution.py:83
  198.9 40.4 %all-to-all-done.3 = bf16[32,32,1024]{2,1,0:T(8,128)(2,1)S(1)} async-done(((bf16[32,32,1024]{2,1,0:T(8,128)(2,1)}), bf16[32,32,1024]{2,1,0:T(8,128)(2,1)S(1)}, u32[]{:S(2)}, u32[]{:S(2)}) %all-to-all-start.3) | async-done | bytes 2097184 | tf_op jit(solution)/shard_map/all_to_all | solution.py:102
  239.3 4.3 %fusion.1 = bf16[1,1024,1024]{2,1,0:T(8,128)(2,1)} fusion(f32[1024,1024]{1,0:T(8,128)} %shard_map.91, bf16[32,32,1024]{2,1,0:T(8,128)(2,1)S(1)} %all-to-all-done.3), kind=kLoop, calls=%fused_computation.4 | loop fusion | flops 3145728 | bytes 8388608 | tf_op jit(solution)/shard_map/broadcast_in_dim | solution.py:128
Async XLA Ops:
  0.0 7.3 %copy-start.6 = (s32[32,4]{0,1:T(4,128)S(1)}, s32[32,4]{0,1:T(4,128)}, u32[]{:S(2)}) copy-start(s32[32,4]{0,1:T(4,128)} %param.14) | copy-start | bytes 1540
  0.0 8.0 %copy-start.2 = (f32[32,4,32]{2,1,0:T(4,128)S(1)}, f32[32,4,32]{2,1,0:T(4,128)}, u32[]{:S(2)}) copy-start(f32[32,4,32]{2,1,0:T(4,128)} %param.15) | copy-start | bytes 49156
  0.0 57.3 %all-to-all-start = ((bf16[32,32,1024]{2,1,0:T(8,128)(2,1)}), bf16[32,32,1024]{2,1,0:T(8,128)(2,1)S(1)}, u32[]{:S(2)}, u32[]{:S(2)}) async-start(bf16[32,32,1024]{2,1,0:T(8,128)(2,1)} %bitcast.18), calls=%async_computation | async-start | bytes 4194304 | tf_op jit(solution)/shard_map/all_to_all | solution.py:102
  57.3 1.3 copy-start
  66.8 52.9 %copy-start.4 = (f32[1,1024]{1,0:T(1,128)S(1)}, f32[1,1024]{1,0:T(1,128)}, u32[]{:S(2)}) copy-start(f32[1,1024]{1,0:T(1,128)} %param.12) | copy-start | bytes 12292
  124.1 2.9 %copy-start.7 = (s32[32,4]{0,1:T(4,128)S(1)}, s32[32,4]{0,1:T(4,128)}, u32[]{:S(2)}) copy-start(s32[32,4]{0,1:T(4,128)} %param.16) | copy-start | bytes 1540
  124.1 3.6 %copy-start.3 = (f32[32,4,32]{2,1,0:T(4,128)S(1)}, f32[32,4,32]{2,1,0:T(4,128)}, u32[]{:S(2)}) copy-start(f32[32,4,32]{2,1,0:T(4,128)} %param.17) | copy-start | bytes 49156
  124.1 52.8 %all-to-all-start.2 = ((bf16[32,32,1024]{2,1,0:T(8,128)(2,1)}), bf16[32,32,1024]{2,1,0:T(8,128)(2,1)S(1)}, u32[]{:S(2)}, u32[]{:S(2)}) async-start(bf16[32,32,1024]{2,1,0:T(8,128)(2,1)} %bitcast.23), calls=%async_computation.2 | async-start | bytes 4194304 | tf_op jit(solution)/shard_map/all_to_all | solution.py:102
  176.9 1.3 copy-start.1
  186.4 2.9 %copy-start.8 = (s32[32]{0:T(128)S(1)}, s32[32]{0:T(128)}, u32[]{:S(2)}) copy-start(s32[32]{0:T(128)} %orders.3) | copy-start | bytes 388
  186.4 3.5 %copy-start.5 = (f32[1,1024]{1,0:T(1,128)S(1)}, f32[1,1024]{1,0:T(1,128)}, u32[]{:S(2)}) copy-start(f32[1,1024]{1,0:T(1,128)} %param.11) | copy-start | bytes 12292
  186.4 52.9 %all-to-all-start.3 = ((bf16[32,32,1024]{2,1,0:T(8,128)(2,1)}), bf16[32,32,1024]{2,1,0:T(8,128)(2,1)S(1)}, u32[]{:S(2)}, u32[]{:S(2)}) async-start(bf16[32,32,1024]{2,1,0:T(8,128)(2,1)} %shard_map.93), calls=%async_computation.3 | async-start | bytes 4194304 | tf_op jit(solution)/shard_map/all_to_all | solution.py:102

commit v2 on v1

--- a/solution.py
+++ b/solution.py
@@ -1,3 +1,4 @@
+import functools
 import math
 
 import jax
@@ -8,40 +9,66 @@
 from jax.sharding import PartitionSpec as P
 
 AXES = ("jown", "pown")
-
-
-def recouple_body(src, orders, first, factors, tiles, mixed):
-    total, rows, width = tiles.shape
+LEAST_ORDER = 512
+
+
+GRANT = 20 * 2**20
+
+
+def in_hbm(x):
+    return pltpu.with_memory_space_constraint(x, pltpu.HBM)
+
+
+def recouple_body(masked, src, orders, first, factors, tiles, mixed):
+    group, rows, width = mixed.shape
     terms = src.shape[1]
+    lanes = min(256, width)
+    base = pl.program_id(0) * group
     row_ids = first[0] + lax.broadcasted_iota(jnp.int32, (rows, 1), 0)
-    col_ids = lax.broadcasted_iota(jnp.int32, (1, width), 1)
-
-    def one(c, carry):
+
+    def one(at_c, carry):
+        c = base + at_c
         own = orders[c]
         weights = factors[c]
-        summed = jnp.zeros((rows, width), jnp.float32)
+        picks, lives, scales = [], [], []
         for k in range(terms):
             pick = src[c, k]
-            live = jnp.minimum(own, orders[pick])
+            live = own if masked else jnp.minimum(own, orders[pick])
             weight = jnp.where(row_ids < live, weights[:, k : k + 1], 0.0)
-            part = weight * tiles[pick].astype(jnp.float32)
-            summed = summed + jnp.where(col_ids < live, part, 0.0)
-        mixed[c] = summed.astype(jnp.bfloat16)
+            picks.append(pick)
+            lives.append(live)
+            scales.append(jnp.broadcast_to(weight, (rows, lanes)))
+        for start in range(0, width, lanes):
+            at = pl.ds(start, lanes)
+            edge = start + lanes > LEAST_ORDER
+            ids = start + lax.broadcasted_iota(jnp.int32, (1, lanes), 1)
+            summed = None
+            for k in range(terms):
+                part = scales[k] * tiles[picks[k], :, at].astype(jnp.float32)
+                if edge and not masked:
+                    part = jnp.where(ids < lives[k], part, 0.0)
+                summed = part if summed is None else summed + part
+            if edge and masked:
+                summed = jnp.where(ids < own, summed, 0.0)
+            mixed[at_c, :, at] = summed.astype(jnp.bfloat16)
         return carry
 
-    lax.fori_loop(0, total, one, 0)
-
-
-def recouple_tiles(tiles, src, factors, orders):
+    lax.fori_loop(0, group, one, 0, unroll=4)
+
+
+def recouple_tiles(tiles, src, factors, orders, masked):
     total, rows, width = tiles.shape
+    group = max(g for g in range(1, total // 4 + 1) if total % g == 0)
     first = (lax.axis_index(AXES) * rows).reshape(1)
     smem = pl.BlockSpec(memory_space=pltpu.SMEM)
     vmem = pl.BlockSpec(memory_space=pltpu.VMEM)
     return pl.pallas_call(
-        recouple_body,
-        out_shape=jax.ShapeDtypeStruct((total, rows, width), jnp.bfloat16),
+        functools.partial(recouple_body, masked),
+        grid=(total // group,),
+        out_shape=pltpu.HBM((total, rows, width), jnp.bfloat16),
         in_specs=[smem, smem, smem, vmem, vmem],
-        out_specs=vmem,
+        out_specs=pl.BlockSpec((group, rows, width), lambda i: (i, 0, 0)),
+        compiler_params=pltpu.CompilerParams(vmem_limit_bytes=GRANT),
         cost_estimate=pl.CostEstimate(
             flops=8 * total * rows * width,
             bytes_accessed=4 * total * rows * width,
@@ -50,8 +77,55 @@
     )(src, orders, first, jnp.swapaxes(factors, 1, 2), tiles)
 
 
+def cycle_body(prop, ph, cycle):
+    rows, width = cycle.shape
+    at = pl.ds(pl.multiple_of(pl.program_id(0) * rows, rows), rows)
+    weighted = (ph[at, :].astype(jnp.float32) * prop[...]).astype(jnp.bfloat16)
+    product = jnp.dot(weighted, ph[...], preferred_element_type=jnp.float32)
+    cycle[...] = (product * (1.0 / math.sqrt(width))).astype(jnp.bfloat16)
+
+
+def cycle_block(prop, ph):
+    width = ph.shape[1]
+    rows = min(256, width)
+    vmem = pl.BlockSpec(memory_space=pltpu.VMEM)
+    return pl.pallas_call(
+        cycle_body,
+        grid=(width // rows,),
+        out_shape=pltpu.HBM(ph.shape, jnp.bfloat16),
+        in_specs=[vmem, vmem],
+        out_specs=pl.BlockSpec((rows, width), lambda i: (i, 0)),
+        compiler_params=pltpu.CompilerParams(vmem_limit_bytes=GRANT),
+        cost_estimate=pl.CostEstimate(
+            flops=2 * ph.size * width, bytes_accessed=4 * ph.size, transcendentals=0
+        ),
+    )(prop, ph)
+
+
+def finish_body(base, returned, updated):
+    total = base[...] + returned[...].astype(jnp.float32)
+    updated[...] = total.astype(jnp.bfloat16)
+
+
+def finish(base, returned):
+    width = base.shape[1]
+    rows = min(512, width)
+    block = pl.BlockSpec((rows, width), lambda i: (i, 0))
+    return pl.pallas_call(
+        finish_body,
+        grid=(width // rows,),
+        out_shape=pltpu.HBM(base.shape, jnp.bfloat16),
+        in_specs=[block, block],
+        out_specs=block,
+        compiler_params=pltpu.CompilerParams(vmem_limit_bytes=GRANT),
+        cost_estimate=pl.CostEstimate(
+            flops=2 * base.size, bytes_accessed=8 * base.size, transcendentals=0
+        ),
+    )(in_hbm(base), in_hbm(returned))
+
+
 def ladder_body(order, bare, vertex, prop, base, scaled):
-    rows, width = base.shape
+    rows, width = bare.shape
     step = pl.program_id(0)
     own = order[0]
     row_ids = lax.broadcasted_iota(jnp.int32, (width, 1), 0)
@@ -83,7 +157,7 @@
     return pl.pallas_call(
         ladder_body,
         grid=(width // rows,),
-        out_shape=jax.ShapeDtypeStruct((width, width), jnp.float32),
+        out_shape=pltpu.HBM((width, width), jnp.float32),
         in_specs=[
             pl.BlockSpec(memory_space=pltpu.SMEM),
             pl.BlockSpec((rows, width), lambda i: (i, 0)),
@@ -92,6 +166,7 @@
         ],
         out_specs=pl.BlockSpec((rows, width), lambda i: (i, 0)),
         scratch_shapes=[pltpu.VMEM((width, width), jnp.bfloat16)],
+        compiler_params=pltpu.CompilerParams(vmem_limit_bytes=GRANT),
         cost_estimate=pl.CostEstimate(
             flops=2 * width**3, bytes_accessed=8 * width * width, transcendentals=0
         ),
@@ -118,14 +193,12 @@
         return tiles.reshape(width, width)
 
     tiles = exchange(to_tiles(vertex[0]))
-    ph = to_block(exchange(recouple_tiles(tiles, pandya_src, pandya_sixj, orders)))
-    weighted = (ph.astype(jnp.float32) * ph_prop).astype(jnp.bfloat16)
-    product = jnp.dot(weighted, ph, preferred_element_type=jnp.float32)
-    cycle = (product * (1.0 / math.sqrt(width))).astype(jnp.bfloat16)
+    ph = to_block(exchange(recouple_tiles(tiles, pandya_src, pandya_sixj, orders, False)))
+    cycle = cycle_block(ph_prop, ph)
     tiles = exchange(to_tiles(cycle))
-    returned = to_block(exchange(recouple_tiles(tiles, back_src, back_sixj, orders)))
+    returned = to_block(exchange(recouple_tiles(tiles, back_src, back_sixj, orders, True)))
     base = ladder_base(own_order, bare[0], vertex[0], pp_prop.reshape(width, 1))
-    return (base + returned.astype(jnp.float32)).astype(jnp.bfloat16)[None]
+    return finish(base, returned)[None]
 
 
 def solution(mesh):

time: 244 us -> 233 us (0.955)
  other arithmetic: 4.9 us -> 0 us
  local copies, waits for them, and re-layouts: 7.76 us -> 3.13 us
  waiting for transfers between devices: 137 us -> 141 us
  matrix products: 3.67 us -> 0 us
  Pallas kernels: 24.4 us -> 21.9 us
    broadcast_in_dim x1 -> x0, other arithmetic: 4.28 us -> none  [per_device(): return (base + returned.astype(jnp.float32)).astype(jnp.bfloat16)[None]]
    all_to_all x3, waiting for transfers between devices: 137 us -> 141 us  [exchange(): return lax.all_to_all(tiles, AXES, split_axis=0, concat_axis=0, tiled=True)]
    unnamed x22, local copies, waits for them, and re-layouts: 6.16 us -> 2.33 us
    dot_general x1 -> x0, matrix products: 3.67 us -> none  [per_device(): product = jnp.dot(weighted, ph, preferred_element_type=jnp.float32)]
    pallas_call x3 -> x5, Pallas kernels: 24.4 us -> 21.9 us  [the longest x2 8.63 us: recouple_tiles(): pl.pallas_call(functools.partial(recouple_body, masked), grid=(total // g...]
  transfers between devices with their start and end apart: 3 -> 3, of which waited for: 3 -> 3; matrix products, arithmetic and copies ran while one was open for 2% -> 1% of each run, Pallas kernels for 3% -> 2%
where the time goes in v2:
time: 233 us
  waiting for transfers between devices  141 us (61%)
  blocking collectives  52.9 us (23%)
  Pallas kernels  21.9 us (9%)
  starting transfers between devices  13.8 us (6%)
  local copies, waits for them, and re-layouts  3.13 us (1%)
    all_to_all x3, waiting for transfers between devices, exchange(): return lax.all_to_all(tiles, AXES, split_axis=0, concat_axis=0, tiled=True)  141 us
    all_to_all x1, blocking collectives, exchange(): return lax.all_to_all(tiles, AXES, split_axis=0, concat_axis=0, tiled=True)  52.9 us
    all_to_all x3, starting transfers between devices, exchange(): return lax.all_to_all(tiles, AXES, split_axis=0, concat_axis=0, tiled=True)  13.8 us
    pallas_call x2, Pallas kernels, recouple_tiles(): pl.pallas_call(functools.partial(recouple_body, masked), grid=(total // g...  8.63 us
    pallas_call x1, Pallas kernels, ladder_base(): pl.pallas_call(ladder_body, grid=(width // rows,), out_shape=pltpu.HBM((w...  5.58 us
  transfers between devices with their start and end apart: 3, of which 3 were waited for; matrix products, arithmetic and copies ran while one was open for 1% of the time, Pallas kernels for 2%

profile of v2, /device:TPU:0, one launch (start us, length us, event | category | flops | bytes accessed | tf_op | source)
XLA Modules:
  0.0 232.9 jit_solution(12283739343259327588)
XLA Ops:
  0.0 0.0 copy-start.7
  0.0 0.0 copy-start.4
  0.0 0.0 copy-start.2
  0.0 7.3 %all-to-all-start = ((bf16[32,32,1024]{2,1,0:T(8,128)(2,1)}), bf16[32,32,1024]{2,1,0:T(8,128)(2,1)S(1)}, u32[]{:S(2)}, u32[]{:S(2)}) async-start(bf16[32,32,1024]{2,1,0:T(8,128)(2,1)} %bitcast.11), calls=%async_computation | async-start | bytes 4194304 | tf_op jit(solution)/shard_map/all_to_all | solution.py:177
  7.4 0.0 copy-done.7
  7.4 0.1 copy.17.src
  7.5 0.0 copy-done.4
  7.5 0.3 copy.16
  7.7 49.6 %all-to-all-done.tiles = bf16[32,32,1024]{2,1,0:T(8,128)(2,1)S(1)} async-done(((bf16[32,32,1024]{2,1,0:T(8,128)(2,1)}), bf16[32,32,1024]{2,1,0:T(8,128)(2,1)S(1)}, u32[]{:S(2)}, u32[]{:S(2)}) %all-to-all-start) | async-done | bytes 2097184 | tf_op jit(solution)/shard_map/all_to_all | solution.py:177
  57.3 0.0 copy-done.2
  57.3 4.5 %shard_map.92 = bf16[32,32,1024]{2,1,0:T(8,128)(2,1)} custom-call(s32[32,4]{1,0:T(8,128)S(1)} %copy.17.src, s32[32]{0:T(128)S(1)} %copy-done.2, s32[1]{0:T(128)} %bitcast.3.first, f32[32,32,4]{2,1,0:T(8,128)S(1)} %bitcast.15, bf16[32,32,1024]{2,1,0:T(8,128)(2,1)S(1)} %all-to-all-done.tiles), custom_call_target="tpu_custom_call" | custom-call | flops 8388608 | bytes 4194304 | tf_op jit(solution)/shard_map/pallas_call | solution.py:65
  61.8 0.0 copy-start.3
  61.8 52.9 %all_to_all.20 = bf16[32,32,1024]{2,1,0:T(8,128)(2,1)S(1)} all-to-all(bf16[32,32,1024]{2,1,0:T(8,128)(2,1)} %shard_map.92), channel_id=1, replica_groups=mesh['jown'=4,'pown'=8] {'jown','pown'}, dimensions={0} | all-to-all | bytes 4194304 | tf_op jit(solution)/shard_map/all_to_all | solution.py:177
  114.7 0.0 copy-done.3
  114.7 3.7 %shard_map.93 = bf16[1024,1024]{1,0:T(8,128)(2,1)} custom-call(f32[1,1024]{1,0:T(1,128)S(1)} %copy-done.3, bf16[1024,1024]{1,0:T(8,128)(2,1)S(1)} %bitcast.14), custom_call_target="tpu_custom_call" | custom-call | flops 2147483648 | bytes 4194304 | tf_op jit(solution)/shard_map/pallas_call | solution.py:92
  118.4 0.0 copy-start.8
  118.4 0.0 copy-start.5
  118.4 2.9 %all-to-all-start.2 = ((bf16[32,32,1024]{2,1,0:T(8,128)(2,1)}), bf16[32,32,1024]{2,1,0:T(8,128)(2,1)S(1)}, u32[]{:S(2)}, u32[]{:S(2)}) async-start(bf16[32,32,1024]{2,1,0:T(8,128)(2,1)} %bitcast.17), calls=%async_computation.2 | async-start | bytes 4194304 | tf_op jit(solution)/shard_map/all_to_all | solution.py:177
  121.3 0.0 copy-done.8
  121.3 0.1 copy.18.src
  121.4 0.0 copy-done.5
  121.4 0.3 copy.15
  121.6 49.6 %all-to-all-done.2.tiles = bf16[32,32,1024]{2,1,0:T(8,128)(2,1)S(1)} async-done(((bf16[32,32,1024]{2,1,0:T(8,128)(2,1)}), bf16[32,32,1024]{2,1,0:T(8,128)(2,1)S(1)}, u32[]{:S(2)}, u32[]{:S(2)}) %all-to-all-start.2) | async-done | bytes 2097184 | tf_op jit(solution)/shard_map/all_to_all | solution.py:177
  171.2 4.2 %shard_map.94 = bf16[32,32,1024]{2,1,0:T(8,128)(2,1)} custom-call(s32[32,4]{1,0:T(8,128)S(1)} %copy.18.src, s32[32]{0:T(128)S(1)} %copy-done.2, s32[1]{0:T(128)} %bitcast.3.first, f32[32,32,4]{2,1,0:T(8,128)S(1)} %bitcast.16, bf16[32,32,1024]{2,1,0:T(8,128)(2,1)S(1)} %all-to-all-done.2.tiles), custom_call_target="tpu_custom_call" | custom-call | flops 8388608 | bytes 4194304 | tf_op jit(solution)/shard_map/pallas_call | solution.py:65
  175.4 0.0 copy-start.6
  175.4 0.0 copy-start
  175.4 3.6 %all-to-all-start.3 = ((bf16[32,32,1024]{2,1,0:T(8,128)(2,1)}), bf16[32,32,1024]{2,1,0:T(8,128)(2,1)}, u32[]{:S(2)}, u32[]{:S(2)}) async-start(bf16[32,32,1024]{2,1,0:T(8,128)(2,1)} %shard_map.94), calls=%async_computation.3 | async-start | bytes 4194304 | tf_op jit(solution)/shard_map/all_to_all | solution.py:177
  179.0 0.6 dynamic_slice.3.order
  179.6 0.0 copy-done.6
  179.6 0.2 copy.14.prop
  179.8 0.0 copy-done
  179.8 0.0 copy-start.1
  179.8 1.6 copy-done.1
  181.4 5.6 %shard_map.91.base = f32[1024,1024]{1,0:T(8,128)} custom-call(s32[1]{0:T(128)} %dynamic_slice.3.order, bf16[1024,1024]{1,0:T(8,128)(2,1)S(1)} %bitcast.13, bf16[1024,1024]{1,0:T(8,128)(2,1)S(1)} %bitcast.12, f32[1024,1]{1,0:T(8,128)S(1)} %copy.14.prop), custom_call_target="tpu_custom_call" | custom-call | flops 2147483648 | bytes 8388608 | tf_op jit(solution)/shard_map/pallas_call | solution.py:157
  187.0 41.9 %all-to-all-done.3 = bf16[32,32,1024]{2,1,0:T(8,128)(2,1)} async-done(((bf16[32,32,1024]{2,1,0:T(8,128)(2,1)}), bf16[32,32,1024]{2,1,0:T(8,128)(2,1)}, u32[]{:S(2)}, u32[]{:S(2)}) %all-to-all-start.3) | async-done | bytes 2097184 | tf_op jit(solution)/shard_map/all_to_all | solution.py:177
  228.9 3.9 %shard_map.95 = bf16[1024,1024]{1,0:T(8,128)(2,1)} custom-call(f32[1024,1024]{1,0:T(8,128)} %shard_map.91.base, bf16[1024,1024]{1,0:T(8,128)(2,1)} %bitcast.9.returned), custom_call_target="tpu_custom_call" | custom-call | flops 2097152 | bytes 8388608 | tf_op jit(solution)/shard_map/pallas_call | solution.py:114
Async XLA Ops:
  0.0 7.4 %copy-start.7 = (s32[32,4]{0,1:T(4,128)S(1)}, s32[32,4]{0,1:T(4,128)}, u32[]{:S(2)}) copy-start(s32[32,4]{0,1:T(4,128)} %param.14) | copy-start | bytes 1540
  0.0 7.5 %copy-start.4 = (f32[32,4,32]{2,1,0:T(4,128)S(1)}, f32[32,4,32]{2,1,0:T(4,128)}, u32[]{:S(2)}) copy-start(f32[32,4,32]{2,1,0:T(4,128)} %param.15) | copy-start | bytes 49156
  0.0 57.3 %copy-start.2 = (s32[32]{0:T(128)S(1)}, s32[32]{0:T(128)}, u32[]{:S(2)}) copy-start(s32[32]{0:T(128)} %orders.3) | copy-start | bytes 388
  0.0 57.3 %all-to-all-start = ((bf16[32,32,1024]{2,1,0:T(8,128)(2,1)}), bf16[32,32,1024]{2,1,0:T(8,128)(2,1)S(1)}, u32[]{:S(2)}, u32[]{:S(2)}) async-start(bf16[32,32,1024]{2,1,0:T(8,128)(2,1)} %bitcast.11), calls=%async_computation | async-start | bytes 4194304 | tf_op jit(solution)/shard_map/all_to_all | solution.py:177
  61.8 52.9 %copy-start.3 = (f32[1,1024]{1,0:T(1,128)S(1)}, f32[1,1024]{1,0:T(1,128)}, u32[]{:S(2)}) copy-start(f32[1,1024]{1,0:T(1,128)} %prop.1) | copy-start | bytes 12292
  118.4 2.9 %copy-start.8 = (s32[32,4]{0,1:T(4,128)S(1)}, s32[32,4]{0,1:T(4,128)}, u32[]{:S(2)}) copy-start(s32[32,4]{0,1:T(4,128)} %param.16) | copy-start | bytes 1540
  118.4 3.0 %copy-start.5 = (f32[32,4,32]{2,1,0:T(4,128)S(1)}, f32[32,4,32]{2,1,0:T(4,128)}, u32[]{:S(2)}) copy-start(f32[32,4,32]{2,1,0:T(4,128)} %param.17) | copy-start | bytes 49156
  118.4 52.8 %all-to-all-start.2 = ((bf16[32,32,1024]{2,1,0:T(8,128)(2,1)}), bf16[32,32,1024]{2,1,0:T(8,128)(2,1)S(1)}, u32[]{:S(2)}, u32[]{:S(2)}) async-start(bf16[32,32,1024]{2,1,0:T(8,128)(2,1)} %bitcast.17), calls=%async_computation.2 | async-start | bytes 4194304 | tf_op jit(solution)/shard_map/all_to_all | solution.py:177
  175.4 4.2 %copy-start.6 = (f32[1,1024]{1,0:T(1,128)S(1)}, f32[1,1024]{1,0:T(1,128)}, u32[]{:S(2)}) copy-start(f32[1,1024]{1,0:T(1,128)} %param.11) | copy-start | bytes 12292
  175.4 4.4 %copy-start = (bf16[1,1024,1024]{2,1,0:T(8,128)(2,1)S(1)}, bf16[1,1024,1024]{2,1,0:T(8,128)(2,1)}, u32[]{:S(2)}) copy-start(bf16[1,1024,1024]{2,1,0:T(8,128)(2,1)} %param.9) | copy-start | bytes 6291460
  175.4 53.5 %all-to-all-start.3 = ((bf16[32,32,1024]{2,1,0:T(8,128)(2,1)}), bf16[32,32,1024]{2,1,0:T(8,128)(2,1)}, u32[]{:S(2)}, u32[]{:S(2)}) async-start(bf16[32,32,1024]{2,1,0:T(8,128)(2,1)} %shard_map.94), calls=%async_computation.3 | async-start | bytes 4194304 | tf_op jit(solution)/shard_map/all_to_all | solution.py:177
  179.8 1.6 copy-start.1

commit v3 on v2

--- a/solution.py
+++ b/solution.py
@@ -8,23 +8,102 @@
 from jax.experimental.pallas import tpu as pltpu
 from jax.sharding import PartitionSpec as P
 
+
 AXES = ("jown", "pown")
 LEAST_ORDER = 512
 
 
 GRANT = 20 * 2**20
+SHARE = 4
 
 
 def in_hbm(x):
     return pltpu.with_memory_space_constraint(x, pltpu.HBM)
 
 
-def recouple_body(masked, src, orders, first, factors, tiles, mixed):
+def digits():
+    low = lax.axis_size("pown").bit_length() - 1
+    high = lax.axis_size("jown").bit_length() - 1
+    assert 1 << low == lax.axis_size("pown") and 1 << high == lax.axis_size("jown")
+    first = list(range(low))[-2:]
+    last = [low] if high else []
+    middle = [b for b in range(low + high) if b not in first + last]
+    return [group for group in (first, middle, last) if group]
+
+
+def place(tile, me, groups):
+    relative = tile ^ me
+    at = relative * 0
+    for group in groups:
+        for bit in reversed(group):
+            at = at * 2 + ((relative >> bit) & 1)
+    return at
+
+
+def small_exchange(tiles, groups):
+    total = tiles.shape[0]
+    sizes = [1 << len(group) for group in groups]
+    tiles = tiles.reshape(*sizes, *tiles.shape[1:])
+    for axis, group in enumerate(groups):
+        got = [lax.index_in_dim(tiles, 0, axis, keepdims=False)]
+        for digit in range(1, sizes[axis]):
+            mask = sum(((digit >> i) & 1) << bit for i, bit in enumerate(group))
+            sent = lax.index_in_dim(tiles, digit, axis, keepdims=False)
+            pairs = [(d, d ^ mask) for d in range(total)]
+            got.append(lax.ppermute(sent, AXES, pairs))
+        tiles = jnp.stack(got, axis)
+    return tiles.reshape(total, *tiles.shape[len(sizes) :])
+
+
+def small_columns(width):
+    return max(128, width // SHARE // 128 * 128)
+
+
+def pack_body(groups, me, block, small, large):
+    columns = small.shape[2]
+    group = block.shape[0]
+
+    def one(t, carry):
+        to = place(pl.program_id(0) * group + t, me[0], groups)
+        small[to] = block[t, :, :columns]
+        large[t] = block[t, :, columns:]
+        return carry
+
+    lax.fori_loop(0, group, one, 0, unroll=4)
+
+
+def pack(me, tiles, groups):
+    total, rows, width = tiles.shape
+    columns = small_columns(width)
+    group = total // 4 if total % 4 == 0 else total
+    return pl.pallas_call(
+        functools.partial(pack_body, groups),
+        grid=(total // group,),
+        out_shape=(
+            pltpu.HBM((total, rows, columns), tiles.dtype),
+            pltpu.HBM((total, rows, width - columns), tiles.dtype),
+        ),
+        in_specs=[
+            pl.BlockSpec(memory_space=pltpu.SMEM),
+            pl.BlockSpec((group, rows, width), lambda i: (i, 0, 0)),
+        ],
+        out_specs=(
+            pl.BlockSpec((total, rows, columns), lambda i: (0, 0, 0)),
+            pl.BlockSpec((group, rows, width - columns), lambda i: (i, 0, 0)),
+        ),
+        compiler_params=pltpu.CompilerParams(vmem_limit_bytes=GRANT),
+        cost_estimate=pl.CostEstimate(
+            flops=0, bytes_accessed=4 * total * rows * width, transcendentals=0
+        ),
+    )(me, tiles)
+
+
+def recouple_body(masked, groups, left, src, orders, me, factors, tiles, mixed):
     group, rows, width = mixed.shape
     terms = src.shape[1]
-    lanes = min(256, width)
+    lanes = 256 if width % 256 == 0 else 128
     base = pl.program_id(0) * group
-    row_ids = first[0] + lax.broadcasted_iota(jnp.int32, (rows, 1), 0)
+    row_ids = me[0] * rows + lax.broadcasted_iota(jnp.int32, (rows, 1), 0)
 
     def one(at_c, carry):
         c = base + at_c
@@ -35,13 +114,14 @@
             pick = src[c, k]
             live = own if masked else jnp.minimum(own, orders[pick])
             weight = jnp.where(row_ids < live, weights[:, k : k + 1], 0.0)
-            picks.append(pick)
+            picks.append(place(pick, me[0], groups) if groups else pick)
             lives.append(live)
             scales.append(jnp.broadcast_to(weight, (rows, lanes)))
+        to = place(c, me[0], groups) if groups else at_c
         for start in range(0, width, lanes):
             at = pl.ds(start, lanes)
-            edge = start + lanes > LEAST_ORDER
-            ids = start + lax.broadcasted_iota(jnp.int32, (1, lanes), 1)
+            edge = left + start + lanes > LEAST_ORDER
+            ids = left + start + lax.broadcasted_iota(jnp.int32, (1, lanes), 1)
             summed = None
             for k in range(terms):
                 part = scales[k] * tiles[picks[k], :, at].astype(jnp.float32)
@@ -50,20 +130,22 @@
                 summed = part if summed is None else summed + part
             if edge and masked:
                 summed = jnp.where(ids < own, summed, 0.0)
-            mixed[at_c, :, at] = summed.astype(jnp.bfloat16)
+            mixed[to, :, at] = summed.astype(jnp.bfloat16)
         return carry
 
     lax.fori_loop(0, group, one, 0, unroll=4)
 
 
-def recouple_tiles(tiles, src, factors, orders, masked):
+def recouple_tiles(me, tiles, src, factors, orders, masked, groups, left):
     total, rows, width = tiles.shape
-    group = max(g for g in range(1, total // 4 + 1) if total % g == 0)
-    first = (lax.axis_index(AXES) * rows).reshape(1)
+    if groups:
+        group = total
+    else:
+        group = max(g for g in range(1, total // 4 + 1) if total % g == 0)
     smem = pl.BlockSpec(memory_space=pltpu.SMEM)
     vmem = pl.BlockSpec(memory_space=pltpu.VMEM)
     return pl.pallas_call(
-        functools.partial(recouple_body, masked),
+        functools.partial(recouple_body, masked, groups, left),
         grid=(total // group,),
         out_shape=pltpu.HBM((total, rows, width), jnp.bfloat16),
         in_specs=[smem, smem, smem, vmem, vmem],
@@ -74,54 +156,98 @@
             bytes_accessed=4 * total * rows * width,
             transcendentals=0,
         ),
-    )(src, orders, first, jnp.swapaxes(factors, 1, 2), tiles)
-
-
-def cycle_body(prop, ph, cycle):
-    rows, width = cycle.shape
-    at = pl.ds(pl.multiple_of(pl.program_id(0) * rows, rows), rows)
+    )(src, orders, me, factors, tiles)
+
+
+def cycle_body(groups, me, prop, small, large, small_out, large_out, ph):
+    step = pl.program_id(0)
+    total, rows, columns = small.shape
+    width = ph.shape[1]
+    group = large_out.shape[0]
+
+    @pl.when(step == 0)
+    def _():
+        def one(t, carry):
+            at = pl.ds(pl.multiple_of(t * rows, rows), rows)
+            ph[at, :columns] = small[place(t, me[0], groups)]
+            ph[at, columns:] = large[t]
+            return carry
+
+        lax.fori_loop(0, total, one, 0, unroll=4)
+
+    height = group * rows
+    at = pl.ds(pl.multiple_of(step * height, height), height)
     weighted = (ph[at, :].astype(jnp.float32) * prop[...]).astype(jnp.bfloat16)
     product = jnp.dot(weighted, ph[...], preferred_element_type=jnp.float32)
-    cycle[...] = (product * (1.0 / math.sqrt(width))).astype(jnp.bfloat16)
-
-
-def cycle_block(prop, ph):
-    width = ph.shape[1]
-    rows = min(256, width)
+    cycle = (product * (1.0 / math.sqrt(width))).astype(jnp.bfloat16)
+    large_out[...] = cycle[:, columns:].reshape(large_out.shape)
+    for t in range(group):
+        to = place(step * group + t, me[0], groups)
+        small_out[to] = cycle[t * rows : (t + 1) * rows, :columns]
+
+
+def cycle_block(me, prop, small, large, groups):
+    total, rows, columns = small.shape
+    width = total * rows
+    group = max(g for g in range(1, total // 4 + 1) if total % g == 0)
     vmem = pl.BlockSpec(memory_space=pltpu.VMEM)
     return pl.pallas_call(
-        cycle_body,
-        grid=(width // rows,),
-        out_shape=pltpu.HBM(ph.shape, jnp.bfloat16),
-        in_specs=[vmem, vmem],
-        out_specs=pl.BlockSpec((rows, width), lambda i: (i, 0)),
-        compiler_params=pltpu.CompilerParams(vmem_limit_bytes=GRANT),
-        cost_estimate=pl.CostEstimate(
-            flops=2 * ph.size * width, bytes_accessed=4 * ph.size, transcendentals=0
-        ),
-    )(prop, ph)
-
-
-def finish_body(base, returned, updated):
-    total = base[...] + returned[...].astype(jnp.float32)
-    updated[...] = total.astype(jnp.bfloat16)
-
-
-def finish(base, returned):
+        functools.partial(cycle_body, groups),
+        grid=(total // group,),
+        out_shape=(
+            pltpu.HBM(small.shape, jnp.bfloat16),
+            pltpu.HBM(large.shape, jnp.bfloat16),
+        ),
+        in_specs=[pl.BlockSpec(memory_space=pltpu.SMEM), vmem, vmem, vmem],
+        out_specs=(
+            pl.BlockSpec(small.shape, lambda i: (0, 0, 0)),
+            pl.BlockSpec((group, rows, width - columns), lambda i: (i, 0, 0)),
+        ),
+        scratch_shapes=[pltpu.VMEM((width, width), jnp.bfloat16)],
+        compiler_params=pltpu.CompilerParams(vmem_limit_bytes=GRANT),
+        cost_estimate=pl.CostEstimate(
+            flops=2 * width**3, bytes_accessed=4 * width * width, transcendentals=0
+        ),
+    )(me, prop, small, large)
+
+
+def finish_body(groups, me, base, small, large, updated):
+    step = pl.program_id(0)
+    group, rows, _ = large.shape
+    columns = small.shape[2]
+
+    def one(t, carry):
+        at = pl.ds(pl.multiple_of(t * rows, rows), rows)
+        part = small[place(step * group + t, me[0], groups)].astype(jnp.float32)
+        updated[at, :columns] = (base[at, :columns] + part).astype(jnp.bfloat16)
+        part = large[t].astype(jnp.float32)
+        updated[at, columns:] = (base[at, columns:] + part).astype(jnp.bfloat16)
+        return carry
+
+    lax.fori_loop(0, group, one, 0, unroll=4)
+
+
+def finish(me, base, small, large, groups):
+    total, rows, columns = small.shape
     width = base.shape[1]
-    rows = min(512, width)
-    block = pl.BlockSpec((rows, width), lambda i: (i, 0))
-    return pl.pallas_call(
-        finish_body,
-        grid=(width // rows,),
+    group = total // 2
+    block = pl.BlockSpec((group * rows, width), lambda i: (i, 0))
+    return pl.pallas_call(
+        functools.partial(finish_body, groups),
+        grid=(total // group,),
         out_shape=pltpu.HBM(base.shape, jnp.bfloat16),
-        in_specs=[block, block],
+        in_specs=[
+            pl.BlockSpec(memory_space=pltpu.SMEM),
+            block,
+            pl.BlockSpec(memory_space=pltpu.VMEM),
+            pl.BlockSpec((group, rows, width - columns), lambda i: (i, 0, 0)),
+        ],
         out_specs=block,
         compiler_params=pltpu.CompilerParams(vmem_limit_bytes=GRANT),
         cost_estimate=pl.CostEstimate(
             flops=2 * base.size, bytes_accessed=8 * base.size, transcendentals=0
         ),
-    )(in_hbm(base), in_hbm(returned))
+    )(me, in_hbm(base), small, in_hbm(large))
 
 
 def ladder_body(order, bare, vertex, prop, base, scaled):
@@ -182,23 +308,31 @@
 ):
     per_owner, width, _ = vertex.shape
     parts = lax.axis_size(AXES)
-    tile_rows = width // parts
+    rows = width // parts
     assert per_owner == 1
-    own_order = lax.dynamic_slice_in_dim(orders, lax.axis_index(AXES), 1)
-
-    def to_tiles(block):
-        return block.reshape(parts, tile_rows, width)
-
-    def to_block(tiles):
-        return tiles.reshape(width, width)
-
-    tiles = exchange(to_tiles(vertex[0]))
-    ph = to_block(exchange(recouple_tiles(tiles, pandya_src, pandya_sixj, orders, False)))
-    cycle = cycle_block(ph_prop, ph)
-    tiles = exchange(to_tiles(cycle))
-    returned = to_block(exchange(recouple_tiles(tiles, back_src, back_sixj, orders, True)))
-    base = ladder_base(own_order, bare[0], vertex[0], pp_prop.reshape(width, 1))
-    return finish(base, returned)[None]
+    groups = digits()
+    me = lax.axis_index(AXES).reshape(1)
+    columns = small_columns(width)
+    own_order = lax.dynamic_slice_in_dim(orders, me[0], 1)
+
+    def recouple(small, large, src, sixj, masked):
+        factors = jnp.swapaxes(sixj, 1, 2)
+        small = small_exchange(small, groups)
+        large = exchange(large)
+        small = recouple_tiles(me, small, src, factors, orders, masked, groups, 0)
+        small = small_exchange(small, groups)
+        large = recouple_tiles(me, large, src, factors, orders, masked, None, columns)
+        large = exchange(large)
+        return small, large
+
+    tiles = vertex[0].reshape(parts, rows, width)
+    small, large = pack(me, tiles, groups)
+    small, large = recouple(small, large, pandya_src, pandya_sixj, False)
+    small, large = cycle_block(me, ph_prop, small, large, groups)
+    small, large = recouple(small, large, back_src, back_sixj, True)
+    prop = pp_prop.reshape(width, 1)
+    base = ladder_base(own_order, bare[0], vertex[0], prop)
+    return finish(me, base, small, large, groups)[None]
 
 
 def solution(mesh):

time: 233 us -> 296 us (1.27)
  waiting for transfers between devices: 141 us -> 208 us
  blocking collectives: 52.9 us -> 0 us
  starting transfers between devices: 13.8 us -> 49.2 us
  Pallas kernels: 21.9 us -> 29.2 us
  local copies, waits for them, and re-layouts: 3.13 us -> 7.37 us
    ppermute x0 -> x28, waiting for transfers between devices: none -> 132 us  [small_exchange(): got.append(lax.ppermute(sent, AXES, pairs))]
    all_to_all x3 -> x4, waiting for transfers between devices: 141 us -> 76.7 us  [exchange(): return lax.all_to_all(tiles, AXES, split_axis=0, concat_axis=0, tiled=True)]
    all_to_all x1 -> x0, blocking collectives: 52.9 us -> none  [exchange(): return lax.all_to_all(tiles, AXES, split_axis=0, concat_axis=0, tiled=True)]
    ppermute x0 -> x28, starting transfers between devices: none -> 32.3 us  [small_exchange(): got.append(lax.ppermute(sent, AXES, pairs))]
    pallas_call x4 -> x7, Pallas kernels: 16.3 us -> 23.6 us  [the longest x4 13.8 us: recouple_tiles(): pl.pallas_call(functools.partial(recouple_body, masked, groups, left), gr...]
    all_to_all x3 -> x4, starting transfers between devices: 13.8 us -> 16.9 us  [exchange(): return lax.all_to_all(tiles, AXES, split_axis=0, concat_axis=0, tiled=True)]
  transfers between devices with their start and end apart: 3 -> 32, of which waited for: 3 -> 23; matrix products, arithmetic and copies ran while one was open for 1% -> 2% of each run, Pallas kernels for 2% -> 4%
where the time goes in v3:
time: 296 us; the launch traced here: 295 us
  waiting for transfers between devices  208 us (70%)
  starting transfers between devices  49.2 us (17%)
  Pallas kernels  29.2 us (10%)
  local copies, waits for them, and re-layouts  7.37 us (2%)
    ppermute x28, waiting for transfers between devices, small_exchange(): got.append(lax.ppermute(sent, AXES, pairs))  132 us
    all_to_all x4, waiting for transfers between devices, exchange(): return lax.all_to_all(tiles, AXES, split_axis=0, concat_axis=0, tiled=True)  76.7 us
    ppermute x28, starting transfers between devices, small_exchange(): got.append(lax.ppermute(sent, AXES, pairs))  32.3 us
    all_to_all x4, starting transfers between devices, exchange(): return lax.all_to_all(tiles, AXES, split_axis=0, concat_axis=0, tiled=True)  16.9 us
    pallas_call x4, Pallas kernels, recouple_tiles(): pl.pallas_call(functools.partial(recouple_body, masked, groups, left), gr...  13.8 us
  transfers between devices with their start and end apart: 32, of which 23 were waited for; matrix products, arithmetic and copies ran while one was open for 2% of the time, Pallas kernels for 4%

profile of v3, /device:TPU:0, one launch (start us, length us, event | category | flops | bytes accessed | tf_op | source)
XLA Modules:
  0.0 295.2 jit_solution(14601262423787541730)
XLA Ops:
  0.0 1.6 copy-done
  1.6 1.9 shard_map.92
  3.5 7.3 %all-to-all-start = ((bf16[32,32,768]{2,1,0:T(8,128)(2,1)}), bf16[32,32,768]{2,1,0:T(8,128)(2,1)S(1)}, u32[]{:S(2)}, u32[]{:S(2)}) async-start(bf16[32,32,768]{2,1,0:T(8,128)(2,1)} %get-tuple-element.10), calls=%async_computation | async-start | bytes 3145728 | tf_op jit(solution)/shard_map/all_to_all | solution.py:303
  10.8 0.1 copy.44.src
  10.9 0.3 copy.38
  11.2 38.3 %all-to-all-done.tiles = bf16[32,32,768]{2,1,0:T(8,128)(2,1)S(1)} async-done(((bf16[32,32,768]{2,1,0:T(8,128)(2,1)}), bf16[32,32,768]{2,1,0:T(8,128)(2,1)S(1)}, u32[]{:S(2)}, u32[]{:S(2)}) %all-to-all-start) | async-done | bytes 1572896 | tf_op jit(solution)/shard_map/all_to_all | solution.py:303
  49.5 4.1 %shard_map.94 = bf16[32,32,768]{2,1,0:T(8,128)(2,1)} custom-call(s32[32,4]{1,0:T(8,128)S(1)} %copy.44.src, s32[32]{0:T(128)S(1)} %copy-done.3, s32[1]{0:T(128)} %bitcast.me, f32[32,32,4]{2,1,0:T(8,128)S(1)} %bitcast.130, bf16[32,32,768]{2,1,0:T(8,128)(2,1)S(1)} %all-to-all-done.tiles), custom_call_target="tpu_custom_call" | custom-call | flops 6291456 | bytes 3145728 | tf_op jit(solution)/shard_map/pallas_call | solution.py:147
  53.6 2.8 all-to-all-start.1
  56.5 3.7 %collective-permute-start.2 = (bf16[4,2,32,256]{3,2,1,0:T(8,128)(2,1)S(1)}, bf16[4,2,32,256]{3,2,1,0:T(8,128)(2,1)S(1)}, u32[]{:S(2)}, u32[]{:S(2)}) collective-permute-start(bf16[4,2,32,256]{3,2,1,0:T(8,128)(2,1)S(1)} %bitcast.171), channel_id=1, source_target_pairs={{0,6},{1,7},{2,4},{3,5},{4,2},{5,3},{6,0},{7,1},{8,14},{9,15},{10,... | collective-permute-start | bytes 393224 | tf_op jit(solution)/shard_map/ppermute | solution.py:53
  60.2 0.8 collective-permute-start
  61.0 28.9 %collective-permute-done.2 = bf16[4,2,32,256]{3,2,1,0:T(8,128)(2,1)S(1)} collective-permute-done((bf16[4,2,32,256]{3,2,1,0:T(8,128)(2,1)S(1)}, bf16[4,2,32,256]{3,2,1,0:T(8,128)(2,1)S(1)}, u32[]{:S(2)}, u32[]{:S(2)}) %collective-permute-start.2) | collective-permute-done | bytes 131104 | tf_op jit(solution)/shard_map/ppermute | solution.py:53
  89.8 15.3 %collective-permute-done.1 = bf16[4,2,32,256]{3,2,1,0:T(8,128)(2,1)S(1)} collective-permute-done((bf16[4,2,32,256]{3,2,1,0:T(8,128)(2,1)S(1)}, bf16[4,2,32,256]{3,2,1,0:T(8,128)(2,1)S(1)}, u32[]{:S(2)}, u32[]{:S(2)}) %collective-permute-start.1) | collective-permute-done | bytes 131104 | tf_op jit(solution)/shard_map/ppermute | solution.py:53
  105.2 2.5 collective-permute-start.5
  107.7 0.5 collective-permute-start.4
  108.2 0.5 collective-permute-start.3
  108.8 2.8 collective-permute-done.5
  111.6 2.4 collective-permute-done.4
  114.2 1.5 collective-permute-done.6
  115.8 3.0 %shard_map.93 = bf16[32,32,256]{2,1,0:T(8,128)(2,1)} custom-call(s32[32,4]{1,0:T(8,128)S(1)} %copy.44.src, s32[32]{0:T(128)S(1)} %copy-done.3, s32[1]{0:T(128)} %bitcast.me, f32[32,32,4]{2,1,0:T(8,128)S(1)} %bitcast.131, bf16[32,32,256]{2,1,0:T(8,128)(2,1)S(1)} %bitcast.136), custom_call_target="tpu_custom_call" | custom-call | flops 2097152 | bytes 1048576 | tf_op jit(solution)/shard_map/pallas_call | solution.py:147
  118.8 1.1 fusion.2
  119.9 1.9 collective-permute-start.9
  121.8 2.5 collective-permute-start.7
  124.3 3.9 %collective-permute-done.9 = bf16[4,2,32,256]{3,2,1,0:T(8,128)(2,1)S(1)} collective-permute-done((bf16[4,2,32,256]{3,2,1,0:T(8,128)(2,1)S(1)}, bf16[4,2,32,256]{3,2,1,0:T(8,128)(2,1)S(1)}, u32[]{:S(2)}, u32[]{:S(2)}) %collective-permute-start.9) | collective-permute-done | bytes 131104 | tf_op jit(solution)/shard_map/ppermute | solution.py:53
  128.3 4.7 %collective-permute-done.8 = bf16[4,2,32,256]{3,2,1,0:T(8,128)(2,1)S(1)} collective-permute-done((bf16[4,2,32,256]{3,2,1,0:T(8,128)(2,1)S(1)}, bf16[4,2,32,256]{3,2,1,0:T(8,128)(2,1)S(1)}, u32[]{:S(2)}, u32[]{:S(2)}) %collective-permute-start.8) | collective-permute-done | bytes 131104 | tf_op jit(solution)/shard_map/ppermute | solution.py:53
  133.1 1.8 collective-permute-start.12
  134.8 1.3 collective-permute-start.11
  136.1 0.5 collective-permute-start.10
  136.6 3.8 %collective-permute-done.12 = bf16[4,2,32,256]{3,2,0,1:T(8,128)(2,1)S(1)} collective-permute-done((bf16[4,2,32,256]{3,2,0,1:T(8,128)(2,1)S(1)}, bf16[4,2,32,256]{3,2,0,1:T(8,128)(2,1)S(1)}, u32[]{:S(2)}, u32[]{:S(2)}) %collective-permute-start.12) | collective-permute-done | bytes 131104 | tf_op jit(solution)/shard_map/ppermute | solution.py:53
  140.4 1.9 collective-permute-done.11
  142.4 0.1 collective-permute-start.13
  142.5 1.5 collective-permute-done.13
  144.0 4.1 %shard_map.95 = (bf16[32,32,256]{2,1,0:T(8,128)(2,1)}, bf16[32,32,768]{2,1,0:T(8,128)(2,1)}) custom-call(s32[1]{0:T(128)} %bitcast.me, f32[1,1024]{1,0:T(1,128)S(1)} %copy-done.4, bf16[32,32,256]{2,1,0:T(8,128)(2,1)S(1)} %bitcast.138, bf16[32,32,768]{2,1,0:T(8,128)(2,1)S(1)} %all-to-all-done.1.large), custom_call_target="tpu_custom_call" | custom-call | flops 2147483648 | bytes 4194304 | tf_op jit(solution)/shard_map/pallas_call | solution.py:194
  148.1 3.2 %all-to-all-start.2 = ((bf16[32,32,768]{2,1,0:T(8,128)(2,1)}), bf16[32,32,768]{2,1,0:T(8,128)(2,1)S(1)}, u32[]{:S(2)}, u32[]{:S(2)}) async-start(bf16[32,32,768]{2,1,0:T(8,128)(2,1)} %get-tuple-element.12), calls=%async_computation.2 | async-start | bytes 3145728 | tf_op jit(solution)/shard_map/all_to_all | solution.py:303
  151.3 0.1 copy.56.src
  151.4 0.3 copy.37
  151.7 38.3 %all-to-all-done.2.tiles = bf16[32,32,768]{2,1,0:T(8,128)(2,1)S(1)} async-done(((bf16[32,32,768]{2,1,0:T(8,128)(2,1)}), bf16[32,32,768]{2,1,0:T(8,128)(2,1)S(1)}, u32[]{:S(2)}, u32[]{:S(2)}) %all-to-all-start.2) | async-done | bytes 1572896 | tf_op jit(solution)/shard_map/all_to_all | solution.py:303
  190.0 3.8 %shard_map.97 = bf16[32,32,768]{2,1,0:T(8,128)(2,1)} custom-call(s32[32,4]{1,0:T(8,128)S(1)} %copy.56.src, s32[32]{0:T(128)S(1)} %copy-done.3, s32[1]{0:T(128)} %bitcast.me, f32[32,32,4]{2,1,0:T(8,128)S(1)} %bitcast.132, bf16[32,32,768]{2,1,0:T(8,128)(2,1)S(1)} %all-to-all-done.2.tiles), custom_call_target="tpu_custom_call" | custom-call | flops 6291456 | bytes 3145728 | tf_op jit(solution)/shard_map/pallas_call | solution.py:147
  193.8 3.5 %all-to-all-start.3 = ((bf16[32,32,768]{2,1,0:T(8,128)(2,1)}), bf16[32,32,768]{2,1,0:T(8,128)(2,1)}, u32[]{:S(2)}, u32[]{:S(2)}) async-start(bf16[32,32,768]{2,1,0:T(8,128)(2,1)} %shard_map.97), calls=%async_computation.3 | async-start | bytes 3145728 | tf_op jit(solution)/shard_map/all_to_all | solution.py:303
  197.4 3.6 %collective-permute-start.16 = (bf16[4,2,32,256]{3,2,1,0:T(8,128)(2,1)S(1)}, bf16[4,2,32,256]{3,2,1,0:T(8,128)(2,1)S(1)}, u32[]{:S(2)}, u32[]{:S(2)}) collective-permute-start(bf16[4,2,32,256]{3,2,1,0:T(8,128)(2,1)S(1)} %bitcast.177), channel_id=1, source_target_pairs={{0,6},{1,7},{2,4},{3,5},{4,2},{5,3},{6,0},{7,1},{8,14},{9,15},{10,... | collective-permute-start | bytes 393224 | tf_op jit(solution)/shard_map/ppermute | solution.py:53
  201.0 0.8 collective-permute-start.14
  201.9 28.8 %collective-permute-done.16 = bf16[4,2,32,256]{3,2,1,0:T(8,128)(2,1)S(1)} collective-permute-done((bf16[4,2,32,256]{3,2,1,0:T(8,128)(2,1)S(1)}, bf16[4,2,32,256]{3,2,1,0:T(8,128)(2,1)S(1)}, u32[]{:S(2)}, u32[]{:S(2)}) %collective-permute-start.16) | collective-permute-done | bytes 131104 | tf_op jit(solution)/shard_map/ppermute | solution.py:53
  230.6 15.3 %collective-permute-done.15 = bf16[4,2,32,256]{3,2,1,0:T(8,128)(2,1)S(1)} collective-permute-done((bf16[4,2,32,256]{3,2,1,0:T(8,128)(2,1)S(1)}, bf16[4,2,32,256]{3,2,1,0:T(8,128)(2,1)S(1)}, u32[]{:S(2)}, u32[]{:S(2)}) %collective-permute-start.15) | collective-permute-done | bytes 131104 | tf_op jit(solution)/shard_map/ppermute | solution.py:53
  246.0 2.5 collective-permute-start.19
  248.5 0.5 collective-permute-start.18
  249.0 0.5 collective-permute-start.17
  249.6 2.8 collective-permute-done.19
  252.4 2.4 collective-permute-done.18
  255.0 1.5 collective-permute-done.20
  256.6 2.9 shard_map.96
  259.5 1.1 fusion
  260.6 1.9 collective-permute-start.23
  262.5 2.5 collective-permute-start.21
  265.1 3.9 %collective-permute-done.23 = bf16[4,2,32,256]{3,2,1,0:T(8,128)(2,1)S(1)} collective-permute-done((bf16[4,2,32,256]{3,2,1,0:T(8,128)(2,1)S(1)}, bf16[4,2,32,256]{3,2,1,0:T(8,128)(2,1)S(1)}, u32[]{:S(2)}, u32[]{:S(2)}) %collective-permute-start.23) | collective-permute-done | bytes 131104 | tf_op jit(solution)/shard_map/ppermute | solution.py:53
  269.0 4.7 %collective-permute-done.22 = bf16[4,2,32,256]{3,2,1,0:T(8,128)(2,1)S(1)} collective-permute-done((bf16[4,2,32,256]{3,2,1,0:T(8,128)(2,1)S(1)}, bf16[4,2,32,256]{3,2,1,0:T(8,128)(2,1)S(1)}, u32[]{:S(2)}, u32[]{:S(2)}) %collective-permute-start.22) | collective-permute-done | bytes 131104 | tf_op jit(solution)/shard_map/ppermute | solution.py:53
  273.8 1.8 collective-permute-start.26
  275.6 1.3 collective-permute-start.25
  276.8 0.5 collective-permute-start.24
  277.4 3.8 %collective-permute-done.26 = bf16[4,2,32,256]{3,2,0,1:T(8,128)(2,1)S(1)} collective-permute-done((bf16[4,2,32,256]{3,2,0,1:T(8,128)(2,1)S(1)}, bf16[4,2,32,256]{3,2,0,1:T(8,128)(2,1)S(1)}, u32[]{:S(2)}, u32[]{:S(2)}) %collective-permute-start.26) | collective-permute-done | bytes 131104 | tf_op jit(solution)/shard_map/ppermute | solution.py:53
  281.1 1.9 collective-permute-done.25
  283.2 0.6 dynamic_slice.3.order
  283.8 0.2 copy.36.prop
  284.1 1.6 copy-done.2
  285.6 5.7 %shard_map.91.base = f32[1024,1024]{1,0:T(8,128)} custom-call(s32[1]{0:T(128)} %dynamic_slice.3.order, bf16[1024,1024]{1,0:T(8,128)(2,1)S(1)} %bitcast.134, bf16[1024,1024]{1,0:T(8,128)(2,1)S(1)} %bitcast.129, f32[1024,1]{1,0:T(8,128)S(1)} %copy.36.prop), custom_call_target="tpu_custom_call" | custom-call | flops 2147483648 | bytes 8388608 | tf_op jit(solution)/shard_map/pallas_call | solution.py:283
  291.4 3.8 %shard_map.98 = bf16[1024,1024]{1,0:T(8,128)(2,1)} custom-call(s32[1]{0:T(128)} %bitcast.me, f32[1024,1024]{1,0:T(8,128)} %shard_map.91.base, bf16[32,32,256]{2,1,0:T(8,128)(2,1)S(1)} %bitcast.135, bf16[32,32,768]{2,1,0:T(8,128)(2,1)} %all-to-all-done.3.large), custom_call_target="tpu_custom_call" | custom-call | flops 2097152 | bytes 8388608 | tf_op jit(solution)/shard_map/pallas_call | solution.py:235
  (62 shorter events, 1.5 us)
Async XLA Ops:
  0.0 1.6 copy-start
  3.5 7.3 %copy-start.10 = (s32[32,4]{0,1:T(4,128)S(1)}, s32[32,4]{0,1:T(4,128)}, u32[]{:S(2)}) copy-start(s32[32,4]{0,1:T(4,128)} %param.14) | copy-start | bytes 1540
  3.5 7.4 %copy-start.7 = (f32[32,4,32]{2,1,0:T(4,128)S(1)}, f32[32,4,32]{2,1,0:T(4,128)}, u32[]{:S(2)}) copy-start(f32[32,4,32]{2,1,0:T(4,128)} %param.15) | copy-start | bytes 49156
  3.5 46.0 %copy-start.3 = (s32[32]{0:T(128)S(1)}, s32[32]{0:T(128)}, u32[]{:S(2)}) copy-start(s32[32]{0:T(128)} %orders.7) | copy-start | bytes 388
  3.5 46.0 %all-to-all-start = ((bf16[32,32,768]{2,1,0:T(8,128)(2,1)}), bf16[32,32,768]{2,1,0:T(8,128)(2,1)S(1)}, u32[]{:S(2)}, u32[]{:S(2)}) async-start(bf16[32,32,768]{2,1,0:T(8,128)(2,1)} %get-tuple-element.10), calls=%async_computation | async-start | bytes 3145728 | tf_op jit(solution)/shard_map/all_to_all | solution.py:303
  53.6 2.8 copy-start.6
  53.6 90.4 %all-to-all-start.1 = ((bf16[32,32,768]{2,1,0:T(8,128)(2,1)}), bf16[32,32,768]{2,1,0:T(8,128)(2,1)S(1)}, u32[]{:S(2)}, u32[]{:S(2)}) async-start(bf16[32,32,768]{2,1,0:T(8,128)(2,1)} %shard_map.94), calls=%async_computation.1 | async-start | bytes 3145728 | tf_op jit(solution)/shard_map/all_to_all | solution.py:303
  56.5 33.3 %collective-permute-start.2 = (bf16[4,2,32,256]{3,2,1,0:T(8,128)(2,1)S(1)}, bf16[4,2,32,256]{3,2,1,0:T(8,128)(2,1)S(1)}, u32[]{:S(2)}, u32[]{:S(2)}) collective-permute-start(bf16[4,2,32,256]{3,2,1,0:T(8,128)(2,1)S(1)} %bitcast.171), channel_id=1, source_target_pairs={{0,6},{1,7},{2,4},{3,5},{4,2},{5,3},{6,0},{7,1},{8,14},{9,15},{10,... | collective-permute-start | bytes 393224 | tf_op jit(solution)/shard_map/ppermute | solution.py:53
  60.2 44.9 %collective-permute-start.1 = (bf16[4,2,32,256]{3,2,1,0:T(8,128)(2,1)S(1)}, bf16[4,2,32,256]{3,2,1,0:T(8,128)(2,1)S(1)}, u32[]{:S(2)}, u32[]{:S(2)}) collective-permute-start(bf16[4,2,32,256]{3,2,1,0:T(8,128)(2,1)S(1)} %bitcast.159), channel_id=1, source_target_pairs={{0,4},{1,5},{2,6},{3,7},{4,0},{5,1},{6,2},{7,3},{8,12},{9,13},{10,... | collective-permute-start | bytes 393224 | tf_op jit(solution)/shard_map/ppermute | solution.py:53
  60.2 44.9 %collective-permute-start = (bf16[4,2,32,256]{3,2,1,0:T(8,128)(2,1)S(1)}, bf16[4,2,32,256]{3,2,1,0:T(8,128)(2,1)S(1)}, u32[]{:S(2)}, u32[]{:S(2)}) collective-permute-start(bf16[4,2,32,256]{3,2,1,0:T(8,128)(2,1)S(1)} %bitcast.147), channel_id=1, source_target_pairs={{0,2},{1,3},{2,0},{3,1},{4,6},{5,7},{6,4},{7,5},{8,10},{9,11},{10,... | collective-permute-start | bytes 393224 | tf_op jit(solution)/shard_map/ppermute | solution.py:53
  105.2 6.4 %collective-permute-start.5 = (bf16[4,2,32,256]{3,2,0,1:T(8,128)(2,1)S(1)}, bf16[4,2,32,256]{3,2,0,1:T(8,128)(2,1)S(1)}, u32[]{:S(2)}, u32[]{:S(2)}) collective-permute-start(bf16[4,2,32,256]{3,2,0,1:T(8,128)(2,1)S(1)} %get-tuple-element.46), channel_id=1, source_target_pairs={{0,17},{1,16},{2,19},{3,18},{4,21},{5,20},{6,23},{7,22},{8,25},{9,... | collective-permute-start | bytes 393224 | tf_op jit(solution)/shard_map/ppermute | solution.py:53
  107.7 6.2 %collective-permute-start.4 = (bf16[4,2,32,256]{3,2,0,1:T(8,128)(2,1)S(1)}, bf16[4,2,32,256]{3,2,0,1:T(8,128)(2,1)S(1)}, u32[]{:S(2)}, u32[]{:S(2)}) collective-permute-start(bf16[4,2,32,256]{3,2,0,1:T(8,128)(2,1)S(1)} %get-tuple-element.47), channel_id=1, source_target_pairs={{0,16},{1,17},{2,18},{3,19},{4,20},{5,21},{6,22},{7,23},{8,24},{9,... | collective-permute-start | bytes 393224 | tf_op jit(solution)/shard_map/ppermute | solution.py:53
  108.2 5.8 %collective-permute-start.3 = (bf16[4,2,32,256]{3,2,0,1:T(8,128)(2,1)S(1)}, bf16[4,2,32,256]{3,2,0,1:T(8,128)(2,1)S(1)}, u32[]{:S(2)}, u32[]{:S(2)}) collective-permute-start(bf16[4,2,32,256]{3,2,0,1:T(8,128)(2,1)S(1)} %get-tuple-element.48), channel_id=1, source_target_pairs={{0,1},{1,0},{2,3},{3,2},{4,5},{5,4},{6,7},{7,6},{8,9},{9,8},{10,11... | collective-permute-start | bytes 393224 | tf_op jit(solution)/shard_map/ppermute | solution.py:53
  114.1 1.6 collective-permute-start.6
  119.9 8.4 %collective-permute-start.9 = (bf16[4,2,32,256]{3,2,1,0:T(8,128)(2,1)S(1)}, bf16[4,2,32,256]{3,2,1,0:T(8,128)(2,1)S(1)}, u32[]{:S(2)}, u32[]{:S(2)}) collective-permute-start(bf16[4,2,32,256]{3,2,1,0:T(8,128)(2,1)S(1)} %bitcast.174), channel_id=1, source_target_pairs={{0,6},{1,7},{2,4},{3,5},{4,2},{5,3},{6,0},{7,1},{8,14},{9,15},{10,... | collective-permute-start | bytes 393224 | tf_op jit(solution)/shard_map/ppermute | solution.py:53
  121.8 11.2 %collective-permute-start.8 = (bf16[4,2,32,256]{3,2,1,0:T(8,128)(2,1)S(1)}, bf16[4,2,32,256]{3,2,1,0:T(8,128)(2,1)S(1)}, u32[]{:S(2)}, u32[]{:S(2)}) collective-permute-start(bf16[4,2,32,256]{3,2,1,0:T(8,128)(2,1)S(1)} %bitcast.162), channel_id=1, source_target_pairs={{0,4},{1,5},{2,6},{3,7},{4,0},{5,1},{6,2},{7,3},{8,12},{9,13},{10,... | collective-permute-start | bytes 393224 | tf_op jit(solution)/shard_map/ppermute | solution.py:53
  121.8 11.2 %collective-permute-start.7 = (bf16[4,2,32,256]{3,2,1,0:T(8,128)(2,1)S(1)}, bf16[4,2,32,256]{3,2,1,0:T(8,128)(2,1)S(1)}, u32[]{:S(2)}, u32[]{:S(2)}) collective-permute-start(bf16[4,2,32,256]{3,2,1,0:T(8,128)(2,1)S(1)} %bitcast.150), channel_id=1, source_target_pairs={{0,2},{1,3},{2,0},{3,1},{4,6},{5,7},{6,4},{7,5},{8,10},{9,11},{10,... | collective-permute-start | bytes 393224 | tf_op jit(solution)/shard_map/ppermute | solution.py:53
  133.1 7.3 %collective-permute-start.12 = (bf16[4,2,32,256]{3,2,0,1:T(8,128)(2,1)S(1)}, bf16[4,2,32,256]{3,2,0,1:T(8,128)(2,1)S(1)}, u32[]{:S(2)}, u32[]{:S(2)}) collective-permute-start(bf16[4,2,32,256]{3,2,0,1:T(8,128)(2,1)S(1)} %get-tuple-element.36), channel_id=1, source_target_pairs={{0,17},{1,16},{2,19},{3,18},{4,21},{5,20},{6,23},{7,22},{8,25},{9,... | collective-permute-start | bytes 393224 | tf_op jit(solution)/shard_map/ppermute | solution.py:53
  134.8 7.4 %collective-permute-start.11 = (bf16[4,2,32,256]{3,2,0,1:T(8,128)(2,1)S(1)}, bf16[4,2,32,256]{3,2,0,1:T(8,128)(2,1)S(1)}, u32[]{:S(2)}, u32[]{:S(2)}) collective-permute-start(bf16[4,2,32,256]{3,2,0,1:T(8,128)(2,1)S(1)} %get-tuple-element.37), channel_id=1, source_target_pairs={{0,16},{1,17},{2,18},{3,19},{4,20},{5,21},{6,22},{7,23},{8,24},{9,... | collective-permute-start | bytes 393224 | tf_op jit(solution)/shard_map/ppermute | solution.py:53
  136.1 6.2 %collective-permute-start.10 = (bf16[4,2,32,256]{3,2,0,1:T(8,128)(2,1)S(1)}, bf16[4,2,32,256]{3,2,0,1:T(8,128)(2,1)S(1)}, u32[]{:S(2)}, u32[]{:S(2)}) collective-permute-start(bf16[4,2,32,256]{3,2,0,1:T(8,128)(2,1)S(1)} %get-tuple-element.38), channel_id=1, source_target_pairs={{0,1},{1,0},{2,3},{3,2},{4,5},{5,4},{6,7},{7,6},{8,9},{9,8},{10,11... | collective-permute-start | bytes 393224 | tf_op jit(solution)/shard_map/ppermute | solution.py:53
  142.3 1.8 copy-start.4
  142.4 1.6 collective-permute-start.13
  148.1 3.2 %copy-start.11 = (s32[32,4]{0,1:T(4,128)S(1)}, s32[32,4]{0,1:T(4,128)}, u32[]{:S(2)}) copy-start(s32[32,4]{0,1:T(4,128)} %param.16) | copy-start | bytes 1540
  148.1 3.3 %copy-start.8 = (f32[32,4,32]{2,1,0:T(4,128)S(1)}, f32[32,4,32]{2,1,0:T(4,128)}, u32[]{:S(2)}) copy-start(f32[32,4,32]{2,1,0:T(4,128)} %param.17) | copy-start | bytes 49156
  148.1 41.9 %all-to-all-start.2 = ((bf16[32,32,768]{2,1,0:T(8,128)(2,1)}), bf16[32,32,768]{2,1,0:T(8,128)(2,1)S(1)}, u32[]{:S(2)}, u32[]{:S(2)}) async-start(bf16[32,32,768]{2,1,0:T(8,128)(2,1)} %get-tuple-element.12), calls=%async_computation.2 | async-start | bytes 3145728 | tf_op jit(solution)/shard_map/all_to_all | solution.py:303
  193.8 3.6 %copy-start.5 = (bf16[32,32,256]{2,1,0:T(8,128)(2,1)S(1)}, bf16[32,32,256]{2,1,0:T(8,128)(2,1)}, u32[]{:S(2)}) copy-start(bf16[32,32,256]{2,1,0:T(8,128)(2,1)} %get-tuple-element.11) | copy-start | bytes 1572868
  193.8 97.6 %all-to-all-start.3 = ((bf16[32,32,768]{2,1,0:T(8,128)(2,1)}), bf16[32,32,768]{2,1,0:T(8,128)(2,1)}, u32[]{:S(2)}, u32[]{:S(2)}) async-start(bf16[32,32,768]{2,1,0:T(8,128)(2,1)} %shard_map.97), calls=%async_computation.3 | async-start | bytes 3145728 | tf_op jit(solution)/shard_map/all_to_all | solution.py:303
  197.4 33.2 %collective-permute-start.16 = (bf16[4,2,32,256]{3,2,1,0:T(8,128)(2,1)S(1)}, bf16[4,2,32,256]{3,2,1,0:T(8,128)(2,1)S(1)}, u32[]{:S(2)}, u32[]{:S(2)}) collective-permute-start(bf16[4,2,32,256]{3,2,1,0:T(8,128)(2,1)S(1)} %bitcast.177), channel_id=1, source_target_pairs={{0,6},{1,7},{2,4},{3,5},{4,2},{5,3},{6,0},{7,1},{8,14},{9,15},{10,... | collective-permute-start | bytes 393224 | tf_op jit(solution)/shard_map/ppermute | solution.py:53
  201.0 44.9 %collective-permute-start.15 = (bf16[4,2,32,256]{3,2,1,0:T(8,128)(2,1)S(1)}, bf16[4,2,32,256]{3,2,1,0:T(8,128)(2,1)S(1)}, u32[]{:S(2)}, u32[]{:S(2)}) collective-permute-start(bf16[4,2,32,256]{3,2,1,0:T(8,128)(2,1)S(1)} %bitcast.165), channel_id=1, source_target_pairs={{0,4},{1,5},{2,6},{3,7},{4,0},{5,1},{6,2},{7,3},{8,12},{9,13},{10,... | collective-permute-start | bytes 393224 | tf_op jit(solution)/shard_map/ppermute | solution.py:53
  201.0 44.9 %collective-permute-start.14 = (bf16[4,2,32,256]{3,2,1,0:T(8,128)(2,1)S(1)}, bf16[4,2,32,256]{3,2,1,0:T(8,128)(2,1)S(1)}, u32[]{:S(2)}, u32[]{:S(2)}) collective-permute-start(bf16[4,2,32,256]{3,2,1,0:T(8,128)(2,1)S(1)} %bitcast.153), channel_id=1, source_target_pairs={{0,2},{1,3},{2,0},{3,1},{4,6},{5,7},{6,4},{7,5},{8,10},{9,11},{10,... | collective-permute-start | bytes 393224 | tf_op jit(solution)/shard_map/ppermute | solution.py:53
  246.0 6.4 %collective-permute-start.19 = (bf16[4,2,32,256]{3,2,0,1:T(8,128)(2,1)S(1)}, bf16[4,2,32,256]{3,2,0,1:T(8,128)(2,1)S(1)}, u32[]{:S(2)}, u32[]{:S(2)}) collective-permute-start(bf16[4,2,32,256]{3,2,0,1:T(8,128)(2,1)S(1)} %get-tuple-element.26), channel_id=1, source_target_pairs={{0,17},{1,16},{2,19},{3,18},{4,21},{5,20},{6,23},{7,22},{8,25},{9,... | collective-permute-start | bytes 393224 | tf_op jit(solution)/shard_map/ppermute | solution.py:53
  248.5 6.2 %collective-permute-start.18 = (bf16[4,2,32,256]{3,2,0,1:T(8,128)(2,1)S(1)}, bf16[4,2,32,256]{3,2,0,1:T(8,128)(2,1)S(1)}, u32[]{:S(2)}, u32[]{:S(2)}) collective-permute-start(bf16[4,2,32,256]{3,2,0,1:T(8,128)(2,1)S(1)} %get-tuple-element.27), channel_id=1, source_target_pairs={{0,16},{1,17},{2,18},{3,19},{4,20},{5,21},{6,22},{7,23},{8,24},{9,... | collective-permute-start | bytes 393224 | tf_op jit(solution)/shard_map/ppermute | solution.py:53
  249.0 5.8 %collective-permute-start.17 = (bf16[4,2,32,256]{3,2,0,1:T(8,128)(2,1)S(1)}, bf16[4,2,32,256]{3,2,0,1:T(8,128)(2,1)S(1)}, u32[]{:S(2)}, u32[]{:S(2)}) collective-permute-start(bf16[4,2,32,256]{3,2,0,1:T(8,128)(2,1)S(1)} %get-tuple-element.28), channel_id=1, source_target_pairs={{0,1},{1,0},{2,3},{3,2},{4,5},{5,4},{6,7},{7,6},{8,9},{9,8},{10,11... | collective-permute-start | bytes 393224 | tf_op jit(solution)/shard_map/ppermute | solution.py:53
  254.9 1.6 collective-permute-start.20
  260.6 8.4 %collective-permute-start.23 = (bf16[4,2,32,256]{3,2,1,0:T(8,128)(2,1)S(1)}, bf16[4,2,32,256]{3,2,1,0:T(8,128)(2,1)S(1)}, u32[]{:S(2)}, u32[]{:S(2)}) collective-permute-start(bf16[4,2,32,256]{3,2,1,0:T(8,128)(2,1)S(1)} %bitcast.180), channel_id=1, source_target_pairs={{0,6},{1,7},{2,4},{3,5},{4,2},{5,3},{6,0},{7,1},{8,14},{9,15},{10,... | collective-permute-start | bytes 393224 | tf_op jit(solution)/shard_map/ppermute | solution.py:53
  262.5 11.2 %collective-permute-start.22 = (bf16[4,2,32,256]{3,2,1,0:T(8,128)(2,1)S(1)}, bf16[4,2,32,256]{3,2,1,0:T(8,128)(2,1)S(1)}, u32[]{:S(2)}, u32[]{:S(2)}) collective-permute-start(bf16[4,2,32,256]{3,2,1,0:T(8,128)(2,1)S(1)} %bitcast.168), channel_id=1, source_target_pairs={{0,4},{1,5},{2,6},{3,7},{4,0},{5,1},{6,2},{7,3},{8,12},{9,13},{10,... | collective-permute-start | bytes 393224 | tf_op jit(solution)/shard_map/ppermute | solution.py:53
  262.5 11.2 %collective-permute-start.21 = (bf16[4,2,32,256]{3,2,1,0:T(8,128)(2,1)S(1)}, bf16[4,2,32,256]{3,2,1,0:T(8,128)(2,1)S(1)}, u32[]{:S(2)}, u32[]{:S(2)}) collective-permute-start(bf16[4,2,32,256]{3,2,1,0:T(8,128)(2,1)S(1)} %bitcast.156), channel_id=1, source_target_pairs={{0,2},{1,3},{2,0},{3,1},{4,6},{5,7},{6,4},{7,5},{8,10},{9,11},{10,... | collective-permute-start | bytes 393224 | tf_op jit(solution)/shard_map/ppermute | solution.py:53
  273.7 10.1 %copy-start.9 = (f32[1,1024]{1,0:T(1,128)S(1)}, f32[1,1024]{1,0:T(1,128)}, u32[]{:S(2)}) copy-start(f32[1,1024]{1,0:T(1,128)} %param.11) | copy-start | bytes 12292
  273.8 10.2 %copy-start.1 = (bf16[1,1024,1024]{2,1,0:T(8,128)(2,1)S(1)}, bf16[1,1024,1024]{2,1,0:T(8,128)(2,1)}, u32[]{:S(2)}) copy-start(bf16[1,1024,1024]{2,1,0:T(8,128)(2,1)} %param.9) | copy-start | bytes 6291460
  273.8 7.3 %collective-permute-start.26 = (bf16[4,2,32,256]{3,2,0,1:T(8,128)(2,1)S(1)}, bf16[4,2,32,256]{3,2,0,1:T(8,128)(2,1)S(1)}, u32[]{:S(2)}, u32[]{:S(2)}) collective-permute-start(bf16[4,2,32,256]{3,2,0,1:T(8,128)(2,1)S(1)} %get-tuple-element.16), channel_id=1, source_target_pairs={{0,17},{1,16},{2,19},{3,18},{4,21},{5,20},{6,23},{7,22},{8,25},{9,... | collective-permute-start | bytes 393224 | tf_op jit(solution)/shard_map/ppermute | solution.py:53
  275.6 7.4 %collective-permute-start.25 = (bf16[4,2,32,256]{3,2,0,1:T(8,128)(2,1)S(1)}, bf16[4,2,32,256]{3,2,0,1:T(8,128)(2,1)S(1)}, u32[]{:S(2)}, u32[]{:S(2)}) collective-permute-start(bf16[4,2,32,256]{3,2,0,1:T(8,128)(2,1)S(1)} %get-tuple-element.17), channel_id=1, source_target_pairs={{0,16},{1,17},{2,18},{3,19},{4,20},{5,21},{6,22},{7,23},{8,24},{9,... | collective-permute-start | bytes 393224 | tf_op jit(solution)/shard_map/ppermute | solution.py:53
  276.8 6.2 %collective-permute-start.24 = (bf16[4,2,32,256]{3,2,0,1:T(8,128)(2,1)S(1)}, bf16[4,2,32,256]{3,2,0,1:T(8,128)(2,1)S(1)}, u32[]{:S(2)}, u32[]{:S(2)}) collective-permute-start(bf16[4,2,32,256]{3,2,0,1:T(8,128)(2,1)S(1)} %get-tuple-element.18), channel_id=1, source_target_pairs={{0,1},{1,0},{2,3},{3,2},{4,5},{5,4},{6,7},{7,6},{8,9},{9,8},{10,11... | collective-permute-start | bytes 393224 | tf_op jit(solution)/shard_map/ppermute | solution.py:53
  283.1 8.2 %collective-permute-start.27 = (bf16[4,4,32,256]{3,2,1,0:T(8,128)(2,1)S(1)}, bf16[4,4,32,256]{3,2,1,0:T(8,128)(2,1)S(1)}, u32[]{:S(2)}, u32[]{:S(2)}) collective-permute-start(bf16[4,4,32,256]{3,2,1,0:T(8,128)(2,1)S(1)} %get-tuple-element.14), channel_id=1, source_target_pairs={{0,8},{1,9},{2,10},{3,11},{4,12},{5,13},{6,14},{7,15},{8,0},{9,1},... | collective-permute-start | bytes 786440 | tf_op jit(solution)/shard_map/ppermute | solution.py:53
  284.0 1.6 copy-start.2

commit v4 on v3

--- a/solution.py
+++ b/solution.py
@@ -40,73 +40,118 @@
     return at
 
 
-def small_exchange(tiles, groups):
-    total = tiles.shape[0]
+def unplace(at, groups):
+    relative = at * 0
+    for group in reversed(groups):
+        for bit in group:
+            relative = relative | ((at & 1) << bit)
+            at = at >> 1
+    return relative
+
+
+def mask_of(digit, group):
+    return sum(((digit >> i) & 1) << bit for i, bit in enumerate(group))
+
+
+def small_exchange(pieces, groups):
+    total = len(pieces) * pieces[0].shape[0]
     sizes = [1 << len(group) for group in groups]
-    tiles = tiles.reshape(*sizes, *tiles.shape[1:])
+    tail = pieces[0].shape[1:]
+    tiles = None
     for axis, group in enumerate(groups):
-        got = [lax.index_in_dim(tiles, 0, axis, keepdims=False)]
-        for digit in range(1, sizes[axis]):
-            mask = sum(((digit >> i) & 1) << bit for i, bit in enumerate(group))
-            sent = lax.index_in_dim(tiles, digit, axis, keepdims=False)
-            pairs = [(d, d ^ mask) for d in range(total)]
-            got.append(lax.ppermute(sent, AXES, pairs))
+        got = []
+        for digit in range(sizes[axis]):
+            if axis:
+                sent = lax.index_in_dim(tiles, digit, axis, keepdims=False)
+            else:
+                sent = pieces[digit].reshape(*sizes[1:], *tail)
+            if digit:
+                mask = mask_of(digit, group)
+                pairs = [(d, d ^ mask) for d in range(total)]
+                sent = lax.ppermute(sent, AXES, pairs)
+            got.append(sent)
         tiles = jnp.stack(got, axis)
-    return tiles.reshape(total, *tiles.shape[len(sizes) :])
+    return tiles.reshape(total, *tail)
 
 
 def small_columns(width):
     return max(128, width // SHARE // 128 * 128)
 
 
-def pack_body(groups, me, block, small, large):
-    columns = small.shape[2]
-    group = block.shape[0]
-
-    def one(t, carry):
-        to = place(pl.program_id(0) * group + t, me[0], groups)
-        small[to] = block[t, :, :columns]
-        large[t] = block[t, :, columns:]
-        return carry
-
-    lax.fori_loop(0, group, one, 0, unroll=4)
-
-
-def pack(me, tiles, groups):
+def scatter(me, groups, pieces, write):
+    for digit, piece in enumerate(pieces):
+        first = mask_of(digit, groups[0])
+
+        def one(q, carry, piece=piece, first=first):
+            write(piece, q, (unplace(q, groups[1:]) | first) ^ me)
+            return carry
+
+        lax.fori_loop(0, piece.shape[0], one, 0, unroll=4)
+
+
+def pieces_of(total, groups, tail):
+    digits_of = 1 << len(groups[0])
+    shape = (total // digits_of, *tail)
+    block = pl.BlockSpec(shape, lambda i: (0,) * len(shape))
+    return (pltpu.HBM(shape, jnp.bfloat16),) * digits_of, (block,) * digits_of
+
+
+def pack_body(groups, me, block, *pieces):
+    def write(piece, q, tile):
+        piece[q] = block[tile]
+
+    scatter(me[0], groups, pieces, write)
+
+
+def pack_small(me, tiles, groups):
     total, rows, width = tiles.shape
     columns = small_columns(width)
-    group = total // 4 if total % 4 == 0 else total
+    shapes, specs = pieces_of(total, groups, (rows, columns))
     return pl.pallas_call(
         functools.partial(pack_body, groups),
-        grid=(total // group,),
-        out_shape=(
-            pltpu.HBM((total, rows, columns), tiles.dtype),
-            pltpu.HBM((total, rows, width - columns), tiles.dtype),
-        ),
+        grid=(1,),
+        out_shape=shapes,
         in_specs=[
             pl.BlockSpec(memory_space=pltpu.SMEM),
-            pl.BlockSpec((group, rows, width), lambda i: (i, 0, 0)),
+            pl.BlockSpec((total, rows, columns), lambda i: (0, 0, 0)),
         ],
-        out_specs=(
-            pl.BlockSpec((total, rows, columns), lambda i: (0, 0, 0)),
-            pl.BlockSpec((group, rows, width - columns), lambda i: (i, 0, 0)),
-        ),
+        out_specs=specs,
+        compiler_params=pltpu.CompilerParams(vmem_limit_bytes=GRANT),
+        cost_estimate=pl.CostEstimate(
+            flops=0, bytes_accessed=4 * total * rows * columns, transcendentals=0
+        ),
+    )(me, in_hbm(tiles))
+
+
+def pack_large_body(block, large):
+    large[...] = block[:, :, block.shape[2] - large.shape[2] :]
+
+
+def pack_large(tiles):
+    total, rows, width = tiles.shape
+    group = total // 2
+    rest = width - small_columns(width)
+    return pl.pallas_call(
+        pack_large_body,
+        grid=(total // group,),
+        out_shape=pltpu.HBM((total, rows, rest), tiles.dtype),
+        in_specs=[pl.BlockSpec((group, rows, width), lambda i: (i, 0, 0))],
+        out_specs=pl.BlockSpec((group, rows, rest), lambda i: (i, 0, 0)),
         compiler_params=pltpu.CompilerParams(vmem_limit_bytes=GRANT),
         cost_estimate=pl.CostEstimate(
             flops=0, bytes_accessed=4 * total * rows * width, transcendentals=0
         ),
-    )(me, tiles)
-
-
-def recouple_body(masked, groups, left, src, orders, me, factors, tiles, mixed):
-    group, rows, width = mixed.shape
+    )(in_hbm(tiles))
+
+
+def recouple_body(masked, groups, left, src, orders, me, factors, tiles, *mixed):
+    width = tiles.shape[2]
+    rows = tiles.shape[1]
     terms = src.shape[1]
     lanes = 256 if width % 256 == 0 else 128
-    base = pl.program_id(0) * group
     row_ids = me[0] * rows + lax.broadcasted_iota(jnp.int32, (rows, 1), 0)
 
-    def one(at_c, carry):
-        c = base + at_c
+    def write(out, to, c):
         own = orders[c]
         weights = factors[c]
         picks, lives, scales = [], [], []
@@ -117,7 +162,6 @@
             picks.append(place(pick, me[0], groups) if groups else pick)
             lives.append(live)
             scales.append(jnp.broadcast_to(weight, (rows, lanes)))
-        to = place(c, me[0], groups) if groups else at_c
         for start in range(0, width, lanes):
             at = pl.ds(start, lanes)
             edge = left + start + lanes > LEAST_ORDER
@@ -130,7 +174,16 @@
                 summed = part if summed is None else summed + part
             if edge and masked:
                 summed = jnp.where(ids < own, summed, 0.0)
-            mixed[to, :, at] = summed.astype(jnp.bfloat16)
+            out[to, :, at] = summed.astype(jnp.bfloat16)
+
+    if groups:
+        scatter(me[0], groups, mixed, write)
+        return
+    group = mixed[0].shape[0]
+    base = pl.program_id(0) * group
+
+    def one(c, carry):
+        write(mixed[0], c, base + c)
         return carry
 
     lax.fori_loop(0, group, one, 0, unroll=4)
@@ -140,16 +193,19 @@
     total, rows, width = tiles.shape
     if groups:
         group = total
+        shapes, specs = pieces_of(total, groups, (rows, width))
     else:
         group = max(g for g in range(1, total // 4 + 1) if total % g == 0)
+        shapes = pltpu.HBM((total, rows, width), jnp.bfloat16)
+        specs = pl.BlockSpec((group, rows, width), lambda i: (i, 0, 0))
     smem = pl.BlockSpec(memory_space=pltpu.SMEM)
     vmem = pl.BlockSpec(memory_space=pltpu.VMEM)
     return pl.pallas_call(
         functools.partial(recouple_body, masked, groups, left),
         grid=(total // group,),
-        out_shape=pltpu.HBM((total, rows, width), jnp.bfloat16),
+        out_shape=shapes,
         in_specs=[smem, smem, smem, vmem, vmem],
-        out_specs=pl.BlockSpec((group, rows, width), lambda i: (i, 0, 0)),
+        out_specs=specs,
         compiler_params=pltpu.CompilerParams(vmem_limit_bytes=GRANT),
         cost_estimate=pl.CostEstimate(
             flops=8 * total * rows * width,
@@ -159,7 +215,8 @@
     )(src, orders, me, factors, tiles)
 
 
-def cycle_body(groups, me, prop, small, large, small_out, large_out, ph):
+def cycle_body(groups, me, prop, small, large, large_out, *rest):
+    pieces, (ph, kept) = rest[:-2], rest[-2:]
     step = pl.program_id(0)
     total, rows, columns = small.shape
     width = ph.shape[1]
@@ -182,8 +239,14 @@
     cycle = (product * (1.0 / math.sqrt(width))).astype(jnp.bfloat16)
     large_out[...] = cycle[:, columns:].reshape(large_out.shape)
     for t in range(group):
-        to = place(step * group + t, me[0], groups)
-        small_out[to] = cycle[t * rows : (t + 1) * rows, :columns]
+        kept[step * group + t] = cycle[t * rows : (t + 1) * rows, :columns]
+
+    @pl.when(step == pl.num_programs(0) - 1)
+    def _():
+        def write(piece, q, tile):
+            piece[q] = kept[tile]
+
+        scatter(me[0], groups, pieces, write)
 
 
 def cycle_block(me, prop, small, large, groups):
@@ -191,24 +254,26 @@
     width = total * rows
     group = max(g for g in range(1, total // 4 + 1) if total % g == 0)
     vmem = pl.BlockSpec(memory_space=pltpu.VMEM)
-    return pl.pallas_call(
+    shapes, specs = pieces_of(total, groups, (rows, columns))
+    large_out, *pieces = pl.pallas_call(
         functools.partial(cycle_body, groups),
         grid=(total // group,),
-        out_shape=(
-            pltpu.HBM(small.shape, jnp.bfloat16),
-            pltpu.HBM(large.shape, jnp.bfloat16),
-        ),
+        out_shape=(pltpu.HBM(large.shape, jnp.bfloat16), *shapes),
         in_specs=[pl.BlockSpec(memory_space=pltpu.SMEM), vmem, vmem, vmem],
         out_specs=(
-            pl.BlockSpec(small.shape, lambda i: (0, 0, 0)),
             pl.BlockSpec((group, rows, width - columns), lambda i: (i, 0, 0)),
-        ),
-        scratch_shapes=[pltpu.VMEM((width, width), jnp.bfloat16)],
+            *specs,
+        ),
+        scratch_shapes=[
+            pltpu.VMEM((width, width), jnp.bfloat16),
+            pltpu.VMEM(small.shape, jnp.bfloat16),
+        ],
         compiler_params=pltpu.CompilerParams(vmem_limit_bytes=GRANT),
         cost_estimate=pl.CostEstimate(
             flops=2 * width**3, bytes_accessed=4 * width * width, transcendentals=0
         ),
     )(me, prop, small, large)
+    return pieces, large_out
 
 
 def finish_body(groups, me, base, small, large, updated):
@@ -326,7 +391,8 @@
         return small, large
 
     tiles = vertex[0].reshape(parts, rows, width)
-    small, large = pack(me, tiles, groups)
+    small = pack_small(me, tiles, groups)
+    large = pack_large(tiles)
     small, large = recouple(small, large, pandya_src, pandya_sixj, False)
     small, large = cycle_block(me, ph_prop, small, large, groups)
     small, large = recouple(small, large, back_src, back_sixj, True)

time: 296 us -> 296 us (level)
  waiting for transfers between devices: 208 us -> 203 us
  local copies, waits for them, and re-layouts: 7.37 us -> 3.49 us
  starting transfers between devices: 49.2 us -> 52.8 us
  Pallas kernels: 29.2 us -> 32.2 us
    ppermute x28, waiting for transfers between devices: 132 us -> 126 us  [small_exchange(): sent = lax.ppermute(sent, AXES, pairs)]
  transfers between devices with their start and end apart: 32 -> 32, of which waited for: 23 -> 25; matrix products, arithmetic and copies ran while one was open for 2% -> 2% of each run, Pallas kernels for 4% -> 5%
where the time goes in v4:
time: 296 us; the launch traced here: 295 us
  waiting for transfers between devices  203 us (69%)
  starting transfers between devices  52.8 us (18%)
  Pallas kernels  32.2 us (11%)
  local copies, waits for them, and re-layouts  3.49 us (1%)
  other arithmetic  3.46 us (1%)
    ppermute x28, waiting for transfers between devices, small_exchange(): sent = lax.ppermute(sent, AXES, pairs)  126 us
    all_to_all x4, waiting for transfers between devices, exchange(): return lax.all_to_all(tiles, AXES, split_axis=0, concat_axis=0, tiled=True)  76.7 us
    ppermute x28, starting transfers between devices, small_exchange(): sent = lax.ppermute(sent, AXES, pairs)  34.8 us
    all_to_all x4, starting transfers between devices, exchange(): return lax.all_to_all(tiles, AXES, split_axis=0, concat_axis=0, tiled=True)  18 us
    pallas_call x4, Pallas kernels, recouple_tiles(): pl.pallas_call(functools.partial(recouple_body, masked, groups, left), gr...  13.8 us
  transfers between devices with their start and end apart: 32, of which 25 were waited for; matrix products, arithmetic and copies ran while one was open for 2% of the time, Pallas kernels for 5%

profile of v4, /device:TPU:0, one launch (start us, length us, event | category | flops | bytes accessed | tf_op | source)
XLA Modules:
  0.0 295.1 jit_solution(11183082301371464082)
XLA Ops:
  0.0 2.5 shard_map.94
  2.5 7.3 %all-to-all-start = ((bf16[32,32,768]{2,1,0:T(8,128)(2,1)}), bf16[32,32,768]{2,1,0:T(8,128)(2,1)S(1)}, u32[]{:S(2)}, u32[]{:S(2)}) async-start(bf16[32,32,768]{2,1,0:T(8,128)(2,1)} %shard_map.94), calls=%async_computation | async-start | bytes 3145728 | tf_op jit(solution)/shard_map/all_to_all | solution.py:368
  9.9 0.3 copy.38
  10.2 38.3 %all-to-all-done.tiles = bf16[32,32,768]{2,1,0:T(8,128)(2,1)S(1)} async-done(((bf16[32,32,768]{2,1,0:T(8,128)(2,1)}), bf16[32,32,768]{2,1,0:T(8,128)(2,1)S(1)}, u32[]{:S(2)}, u32[]{:S(2)}) %all-to-all-start) | async-done | bytes 1572896 | tf_op jit(solution)/shard_map/all_to_all | solution.py:368
  48.5 4.1 %shard_map.95 = bf16[32,32,768]{2,1,0:T(8,128)(2,1)} custom-call(s32[32,4]{1,0:T(8,128)S(1)} %copy.44.src, s32[32]{0:T(128)S(1)} %copy-done.2, s32[1]{0:T(128)} %bitcast.me, f32[32,32,4]{2,1,0:T(8,128)S(1)} %bitcast.131, bf16[32,32,768]{2,1,0:T(8,128)(2,1)S(1)} %all-to-all-done.tiles), custom_call_target="tpu_custom_call" | custom-call | flops 6291456 | bytes 3145728 | tf_op jit(solution)/shard_map/pallas_call | solution.py:203
  52.6 2.7 all-to-all-start.1
  55.3 2.0 shard_map.92
  57.3 1.7 collective-permute-start
  59.0 2.5 collective-permute-start.1
  61.7 22.9 %collective-permute-done = bf16[4,2,32,256]{3,2,1,0:T(8,128)(2,1)S(1)} collective-permute-done((bf16[4,2,32,256]{3,2,1,0:T(8,128)(2,1)}, bf16[4,2,32,256]{3,2,1,0:T(8,128)(2,1)S(1)}, u32[]{:S(2)}, u32[]{:S(2)}) %collective-permute-start) | collective-permute-done | bytes 131104 | tf_op jit(solution)/shard_map/ppermute | solution.py:71
  84.5 17.2 %collective-permute-done.1 = bf16[4,2,32,256]{3,2,1,0:T(8,128)(2,1)S(1)} collective-permute-done((bf16[4,2,32,256]{3,2,1,0:T(8,128)(2,1)}, bf16[4,2,32,256]{3,2,1,0:T(8,128)(2,1)S(1)}, u32[]{:S(2)}, u32[]{:S(2)}) %collective-permute-start.1) | collective-permute-done | bytes 131104 | tf_op jit(solution)/shard_map/ppermute | solution.py:71
  101.7 1.0 pad_maximum_fusion
  102.7 2.5 collective-permute-start.5
  105.2 0.5 collective-permute-start.4
  105.7 0.5 collective-permute-start.3
  106.3 3.4 %collective-permute-done.5 = bf16[4,2,32,256]{3,2,0,1:T(8,128)(2,1)S(1)} collective-permute-done((bf16[4,2,32,256]{3,2,0,1:T(8,128)(2,1)S(1)}, bf16[4,2,32,256]{3,2,0,1:T(8,128)(2,1)S(1)}, u32[]{:S(2)}, u32[]{:S(2)}) %collective-permute-start.5) | collective-permute-done | bytes 131104 | tf_op jit(solution)/shard_map/ppermute | solution.py:71
  109.7 1.2 collective-permute-done.4
  111.2 1.5 collective-permute-done.6
  112.7 3.0 %shard_map.93 = (bf16[8,32,256]{2,1,0:T(8,128)(2,1)}, bf16[8,32,256]{2,1,0:T(8,128)(2,1)}, bf16[8,32,256]{2,1,0:T(8,128)(2,1)}, bf16[8,32,256]{2,1,0:T(8,128)(2,1)}) custom-call(s32[32,4]{1,0:T(8,128)S(1)} %copy.44.src, s32[32]{0:T(128)S(1)} %copy-done.2, s32[1]{0:T(128)} %bitcast.me, f32[32,32,4]{2,1,0:T(8,128)S(1)} %bitcast.132, ...), custom_call_target="tpu_custom_call" | custom-call | flops 2097152 | bytes 1048576 | tf_op jit(solution)/shard_map/pallas_call | solution.py:203
  115.8 3.3 %collective-permute-start.7 = (bf16[4,2,32,256]{3,2,1,0:T(8,128)(2,1)}, bf16[4,2,32,256]{3,2,1,0:T(8,128)(2,1)S(1)}, u32[]{:S(2)}, u32[]{:S(2)}) collective-permute-start(bf16[4,2,32,256]{3,2,1,0:T(8,128)(2,1)} %bitcast.182), channel_id=1, source_target_pairs={{0,2},{1,3},{2,0},{3,1},{4,6},{5,7},{6,4},{7,5},{8,10},{9,11},{10,... | collective-permute-start | bytes 393224 | tf_op jit(solution)/shard_map/ppermute | solution.py:71
  119.1 0.4 collective-permute-start.8
  119.5 2.0 collective-permute-start.9
  121.5 3.1 %collective-permute-done.7 = bf16[4,2,32,256]{3,2,1,0:T(8,128)(2,1)S(1)} collective-permute-done((bf16[4,2,32,256]{3,2,1,0:T(8,128)(2,1)}, bf16[4,2,32,256]{3,2,1,0:T(8,128)(2,1)S(1)}, u32[]{:S(2)}, u32[]{:S(2)}) %collective-permute-start.7) | collective-permute-done | bytes 131104 | tf_op jit(solution)/shard_map/ppermute | solution.py:71
  124.6 7.6 %collective-permute-done.8 = bf16[4,2,32,256]{3,2,1,0:T(8,128)(2,1)S(1)} collective-permute-done((bf16[4,2,32,256]{3,2,1,0:T(8,128)(2,1)}, bf16[4,2,32,256]{3,2,1,0:T(8,128)(2,1)S(1)}, u32[]{:S(2)}, u32[]{:S(2)}) %collective-permute-start.8) | collective-permute-done | bytes 131104 | tf_op jit(solution)/shard_map/ppermute | solution.py:71
  132.2 1.0 pad_maximum_fusion.3
  133.2 1.8 collective-permute-start.12
  135.0 1.3 collective-permute-start.11
  136.3 0.5 collective-permute-start.10
  136.8 2.4 collective-permute-done.12
  139.2 1.3 collective-permute-done.11
  140.6 0.7 collective-permute-done.10
  141.4 1.5 collective-permute-done.13
  143.0 4.4 %shard_map.96 = (bf16[32,32,768]{2,1,0:T(8,128)(2,1)}, bf16[8,32,256]{2,1,0:T(8,128)(2,1)}, bf16[8,32,256]{2,1,0:T(8,128)(2,1)}, bf16[8,32,256]{2,1,0:T(8,128)(2,1)}, bf16[8,32,256]{2,1,0:T(8,128)(2,1)}) custom-call(s32[1]{0:T(128)} %bitcast.me, f32[1,1024]{1,0:T(1,128)S(1)} %copy-done.3, bf16[32,32,256]{2,1,0:T(8,128)(2,1)S(1)} %bitcast.139, ...), custom_call_target="tpu_custom_call" | custom-call | flops 2147483648 | bytes 4194304 | tf_op jit(solution)/shard_map/pallas_call | solution.py:258
  147.5 4.4 %all-to-all-start.2 = ((bf16[32,32,768]{2,1,0:T(8,128)(2,1)}), bf16[32,32,768]{2,1,0:T(8,128)(2,1)S(1)}, u32[]{:S(2)}, u32[]{:S(2)}) async-start(bf16[32,32,768]{2,1,0:T(8,128)(2,1)} %get-tuple-element.38), calls=%async_computation.2 | async-start | bytes 3145728 | tf_op jit(solution)/shard_map/all_to_all | solution.py:368
  152.3 38.3 %all-to-all-done.2.tiles = bf16[32,32,768]{2,1,0:T(8,128)(2,1)S(1)} async-done(((bf16[32,32,768]{2,1,0:T(8,128)(2,1)}), bf16[32,32,768]{2,1,0:T(8,128)(2,1)S(1)}, u32[]{:S(2)}, u32[]{:S(2)}) %all-to-all-start.2) | async-done | bytes 1572896 | tf_op jit(solution)/shard_map/all_to_all | solution.py:368
  190.6 3.8 %shard_map.98 = bf16[32,32,768]{2,1,0:T(8,128)(2,1)} custom-call(s32[32,4]{1,0:T(8,128)S(1)} %copy.56.src, s32[32]{0:T(128)S(1)} %copy-done.2, s32[1]{0:T(128)} %bitcast.me, f32[32,32,4]{2,1,0:T(8,128)S(1)} %bitcast.133, bf16[32,32,768]{2,1,0:T(8,128)(2,1)S(1)} %all-to-all-done.2.tiles), custom_call_target="tpu_custom_call" | custom-call | flops 6291456 | bytes 3145728 | tf_op jit(solution)/shard_map/pallas_call | solution.py:203
  194.4 3.6 %all-to-all-start.3 = ((bf16[32,32,768]{2,1,0:T(8,128)(2,1)}), bf16[32,32,768]{2,1,0:T(8,128)(2,1)}, u32[]{:S(2)}, u32[]{:S(2)}) async-start(bf16[32,32,768]{2,1,0:T(8,128)(2,1)} %shard_map.98), calls=%async_computation.3 | async-start | bytes 3145728 | tf_op jit(solution)/shard_map/all_to_all | solution.py:368
  198.0 1.7 collective-permute-start.14
  199.7 2.5 collective-permute-start.15
  202.4 24.6 %collective-permute-done.14 = bf16[4,2,32,256]{3,2,1,0:T(8,128)(2,1)S(1)} collective-permute-done((bf16[4,2,32,256]{3,2,1,0:T(8,128)(2,1)S(1)}, bf16[4,2,32,256]{3,2,1,0:T(8,128)(2,1)S(1)}, u32[]{:S(2)}, u32[]{:S(2)}) %collective-permute-start.14) | collective-permute-done | bytes 131104 | tf_op jit(solution)/shard_map/ppermute | solution.py:71
  227.0 17.3 %collective-permute-done.15 = bf16[4,2,32,256]{3,2,1,0:T(8,128)(2,1)S(1)} collective-permute-done((bf16[4,2,32,256]{3,2,1,0:T(8,128)(2,1)S(1)}, bf16[4,2,32,256]{3,2,1,0:T(8,128)(2,1)S(1)}, u32[]{:S(2)}, u32[]{:S(2)}) %collective-permute-start.15) | collective-permute-done | bytes 131104 | tf_op jit(solution)/shard_map/ppermute | solution.py:71
  244.4 2.5 collective-permute-start.19
  246.9 0.5 collective-permute-start.18
  247.4 0.5 collective-permute-start.17
  248.0 3.4 %collective-permute-done.19 = bf16[4,2,32,256]{3,2,0,1:T(8,128)(2,1)S(1)} collective-permute-done((bf16[4,2,32,256]{3,2,0,1:T(8,128)(2,1)S(1)}, bf16[4,2,32,256]{3,2,0,1:T(8,128)(2,1)S(1)}, u32[]{:S(2)}, u32[]{:S(2)}) %collective-permute-start.19) | collective-permute-done | bytes 131104 | tf_op jit(solution)/shard_map/ppermute | solution.py:71
  251.3 1.2 collective-permute-done.18
  252.8 1.5 collective-permute-done.20
  254.4 2.9 shard_map.97
  257.3 3.3 %collective-permute-start.21 = (bf16[4,2,32,256]{3,2,1,0:T(8,128)(2,1)}, bf16[4,2,32,256]{3,2,1,0:T(8,128)(2,1)S(1)}, u32[]{:S(2)}, u32[]{:S(2)}) collective-permute-start(bf16[4,2,32,256]{3,2,1,0:T(8,128)(2,1)} %bitcast.183), channel_id=1, source_target_pairs={{0,2},{1,3},{2,0},{3,1},{4,6},{5,7},{6,4},{7,5},{8,10},{9,11},{10,... | collective-permute-start | bytes 393224 | tf_op jit(solution)/shard_map/ppermute | solution.py:71
  260.7 0.4 collective-permute-start.22
  261.1 2.0 collective-permute-start.23
  263.1 3.1 %collective-permute-done.21 = bf16[4,2,32,256]{3,2,1,0:T(8,128)(2,1)S(1)} collective-permute-done((bf16[4,2,32,256]{3,2,1,0:T(8,128)(2,1)}, bf16[4,2,32,256]{3,2,1,0:T(8,128)(2,1)S(1)}, u32[]{:S(2)}, u32[]{:S(2)}) %collective-permute-start.21) | collective-permute-done | bytes 131104 | tf_op jit(solution)/shard_map/ppermute | solution.py:71
  266.2 7.6 %collective-permute-done.22 = bf16[4,2,32,256]{3,2,1,0:T(8,128)(2,1)S(1)} collective-permute-done((bf16[4,2,32,256]{3,2,1,0:T(8,128)(2,1)}, bf16[4,2,32,256]{3,2,1,0:T(8,128)(2,1)S(1)}, u32[]{:S(2)}, u32[]{:S(2)}) %collective-permute-start.22) | collective-permute-done | bytes 131104 | tf_op jit(solution)/shard_map/ppermute | solution.py:71
  273.8 1.0 pad_maximum_fusion.9
  274.8 1.8 collective-permute-start.26
  276.6 1.3 collective-permute-start.25
  277.9 0.5 collective-permute-start.24
  278.4 2.4 collective-permute-done.26
  280.8 1.3 collective-permute-done.25
  282.2 0.7 collective-permute-done.24
  283.0 0.6 dynamic_slice.3.order
  283.9 1.6 copy-done.1
  285.5 5.7 %shard_map.91.base = f32[1024,1024]{1,0:T(8,128)} custom-call(s32[1]{0:T(128)} %dynamic_slice.3.order, bf16[1024,1024]{1,0:T(8,128)(2,1)S(1)} %bitcast.135, bf16[1024,1024]{1,0:T(8,128)(2,1)S(1)} %bitcast.130, f32[1024,1]{1,0:T(8,128)S(1)} %copy.36.prop), custom_call_target="tpu_custom_call" | custom-call | flops 2147483648 | bytes 8388608 | tf_op jit(solution)/shard_map/pallas_call | solution.py:348
  291.2 3.8 %shard_map.99 = bf16[1024,1024]{1,0:T(8,128)(2,1)} custom-call(s32[1]{0:T(128)} %bitcast.me, f32[1024,1024]{1,0:T(8,128)} %shard_map.91.base, bf16[32,32,256]{2,1,0:T(8,128)(2,1)S(1)} %bitcast.136, bf16[32,32,768]{2,1,0:T(8,128)(2,1)} %all-to-all-done.3.large), custom_call_target="tpu_custom_call" | custom-call | flops 2097152 | bytes 8388608 | tf_op jit(solution)/shard_map/pallas_call | solution.py:300
  (61 shorter events, 2.5 us)
Async XLA Ops:
  2.5 7.3 %copy-start.8 = (s32[32,4]{0,1:T(4,128)S(1)}, s32[32,4]{0,1:T(4,128)}, u32[]{:S(2)}) copy-start(s32[32,4]{0,1:T(4,128)} %param.14) | copy-start | bytes 1540
  2.5 7.4 %copy-start.5 = (f32[32,4,32]{2,1,0:T(4,128)S(1)}, f32[32,4,32]{2,1,0:T(4,128)}, u32[]{:S(2)}) copy-start(f32[32,4,32]{2,1,0:T(4,128)} %param.15) | copy-start | bytes 49156
  2.5 46.0 %copy-start.2 = (s32[32]{0:T(128)S(1)}, s32[32]{0:T(128)}, u32[]{:S(2)}) copy-start(s32[32]{0:T(128)} %orders.7) | copy-start | bytes 388
  2.5 46.0 %all-to-all-start = ((bf16[32,32,768]{2,1,0:T(8,128)(2,1)}), bf16[32,32,768]{2,1,0:T(8,128)(2,1)S(1)}, u32[]{:S(2)}, u32[]{:S(2)}) async-start(bf16[32,32,768]{2,1,0:T(8,128)(2,1)} %shard_map.94), calls=%async_computation | async-start | bytes 3145728 | tf_op jit(solution)/shard_map/all_to_all | solution.py:368
  52.6 90.4 %all-to-all-start.1 = ((bf16[32,32,768]{2,1,0:T(8,128)(2,1)}), bf16[32,32,768]{2,1,0:T(8,128)(2,1)S(1)}, u32[]{:S(2)}, u32[]{:S(2)}) async-start(bf16[32,32,768]{2,1,0:T(8,128)(2,1)} %shard_map.95), calls=%async_computation.1 | async-start | bytes 3145728 | tf_op jit(solution)/shard_map/all_to_all | solution.py:368
  57.3 27.3 %collective-permute-start = (bf16[4,2,32,256]{3,2,1,0:T(8,128)(2,1)}, bf16[4,2,32,256]{3,2,1,0:T(8,128)(2,1)S(1)}, u32[]{:S(2)}, u32[]{:S(2)}) collective-permute-start(bf16[4,2,32,256]{3,2,1,0:T(8,128)(2,1)} %bitcast.184), channel_id=1, source_target_pairs={{0,2},{1,3},{2,0},{3,1},{4,6},{5,7},{6,4},{7,5},{8,10},{9,11},{10,... | collective-permute-start | bytes 393224 | tf_op jit(solution)/shard_map/ppermute | solution.py:71
  59.0 42.7 %collective-permute-start.1 = (bf16[4,2,32,256]{3,2,1,0:T(8,128)(2,1)}, bf16[4,2,32,256]{3,2,1,0:T(8,128)(2,1)S(1)}, u32[]{:S(2)}, u32[]{:S(2)}) collective-permute-start(bf16[4,2,32,256]{3,2,1,0:T(8,128)(2,1)} %bitcast.181), channel_id=1, source_target_pairs={{0,4},{1,5},{2,6},{3,7},{4,0},{5,1},{6,2},{7,3},{8,12},{9,13},{10,... | collective-permute-start | bytes 393224 | tf_op jit(solution)/shard_map/ppermute | solution.py:71
  61.5 40.2 %collective-permute-start.2 = (bf16[4,2,32,256]{3,2,1,0:T(8,128)(2,1)}, bf16[4,2,32,256]{3,2,1,0:T(8,128)(2,1)S(1)}, u32[]{:S(2)}, u32[]{:S(2)}) collective-permute-start(bf16[4,2,32,256]{3,2,1,0:T(8,128)(2,1)} %bitcast.178), channel_id=1, source_target_pairs={{0,6},{1,7},{2,4},{3,5},{4,2},{5,3},{6,0},{7,1},{8,14},{9,15},{10,... | collective-permute-start | bytes 393224 | tf_op jit(solution)/shard_map/ppermute | solution.py:71
  102.7 6.9 %collective-permute-start.5 = (bf16[4,2,32,256]{3,2,0,1:T(8,128)(2,1)S(1)}, bf16[4,2,32,256]{3,2,0,1:T(8,128)(2,1)S(1)}, u32[]{:S(2)}, u32[]{:S(2)}) collective-permute-start(bf16[4,2,32,256]{3,2,0,1:T(8,128)(2,1)S(1)} %get-tuple-element.60), channel_id=1, source_target_pairs={{0,17},{1,16},{2,19},{3,18},{4,21},{5,20},{6,23},{7,22},{8,25},{9,... | collective-permute-start | bytes 393224 | tf_op jit(solution)/shard_map/ppermute | solution.py:71
  105.2 5.7 %collective-permute-start.4 = (bf16[4,2,32,256]{3,2,0,1:T(8,128)(2,1)S(1)}, bf16[4,2,32,256]{3,2,0,1:T(8,128)(2,1)S(1)}, u32[]{:S(2)}, u32[]{:S(2)}) collective-permute-start(bf16[4,2,32,256]{3,2,0,1:T(8,128)(2,1)S(1)} %get-tuple-element.61), channel_id=1, source_target_pairs={{0,16},{1,17},{2,18},{3,19},{4,20},{5,21},{6,22},{7,23},{8,24},{9,... | collective-permute-start | bytes 393224 | tf_op jit(solution)/shard_map/ppermute | solution.py:71
  105.7 5.2 %collective-permute-start.3 = (bf16[4,2,32,256]{3,2,0,1:T(8,128)(2,1)S(1)}, bf16[4,2,32,256]{3,2,0,1:T(8,128)(2,1)S(1)}, u32[]{:S(2)}, u32[]{:S(2)}) collective-permute-start(bf16[4,2,32,256]{3,2,0,1:T(8,128)(2,1)S(1)} %get-tuple-element.62), channel_id=1, source_target_pairs={{0,1},{1,0},{2,3},{3,2},{4,5},{5,4},{6,7},{7,6},{8,9},{9,8},{10,11... | collective-permute-start | bytes 393224 | tf_op jit(solution)/shard_map/ppermute | solution.py:71
  111.1 1.6 collective-permute-start.6
  115.8 8.9 %collective-permute-start.7 = (bf16[4,2,32,256]{3,2,1,0:T(8,128)(2,1)}, bf16[4,2,32,256]{3,2,1,0:T(8,128)(2,1)S(1)}, u32[]{:S(2)}, u32[]{:S(2)}) collective-permute-start(bf16[4,2,32,256]{3,2,1,0:T(8,128)(2,1)} %bitcast.182), channel_id=1, source_target_pairs={{0,2},{1,3},{2,0},{3,1},{4,6},{5,7},{6,4},{7,5},{8,10},{9,11},{10,... | collective-permute-start | bytes 393224 | tf_op jit(solution)/shard_map/ppermute | solution.py:71
  119.1 13.1 %collective-permute-start.8 = (bf16[4,2,32,256]{3,2,1,0:T(8,128)(2,1)}, bf16[4,2,32,256]{3,2,1,0:T(8,128)(2,1)S(1)}, u32[]{:S(2)}, u32[]{:S(2)}) collective-permute-start(bf16[4,2,32,256]{3,2,1,0:T(8,128)(2,1)} %bitcast.179), channel_id=1, source_target_pairs={{0,4},{1,5},{2,6},{3,7},{4,0},{5,1},{6,2},{7,3},{8,12},{9,13},{10,... | collective-permute-start | bytes 393224 | tf_op jit(solution)/shard_map/ppermute | solution.py:71
  119.5 12.7 %collective-permute-start.9 = (bf16[4,2,32,256]{3,2,1,0:T(8,128)(2,1)}, bf16[4,2,32,256]{3,2,1,0:T(8,128)(2,1)S(1)}, u32[]{:S(2)}, u32[]{:S(2)}) collective-permute-start(bf16[4,2,32,256]{3,2,1,0:T(8,128)(2,1)} %bitcast.176), channel_id=1, source_target_pairs={{0,6},{1,7},{2,4},{3,5},{4,2},{5,3},{6,0},{7,1},{8,14},{9,15},{10,... | collective-permute-start | bytes 393224 | tf_op jit(solution)/shard_map/ppermute | solution.py:71
  133.2 6.0 %collective-permute-start.12 = (bf16[4,2,32,256]{3,2,0,1:T(8,128)(2,1)S(1)}, bf16[4,2,32,256]{3,2,0,1:T(8,128)(2,1)S(1)}, u32[]{:S(2)}, u32[]{:S(2)}) collective-permute-start(bf16[4,2,32,256]{3,2,0,1:T(8,128)(2,1)S(1)} %get-tuple-element.54), channel_id=1, source_target_pairs={{0,17},{1,16},{2,19},{3,18},{4,21},{5,20},{6,23},{7,22},{8,25},{9,... | collective-permute-start | bytes 393224 | tf_op jit(solution)/shard_map/ppermute | solution.py:71
  135.0 5.6 %collective-permute-start.11 = (bf16[4,2,32,256]{3,2,0,1:T(8,128)(2,1)S(1)}, bf16[4,2,32,256]{3,2,0,1:T(8,128)(2,1)S(1)}, u32[]{:S(2)}, u32[]{:S(2)}) collective-permute-start(bf16[4,2,32,256]{3,2,0,1:T(8,128)(2,1)S(1)} %get-tuple-element.55), channel_id=1, source_target_pairs={{0,16},{1,17},{2,18},{3,19},{4,20},{5,21},{6,22},{7,23},{8,24},{9,... | collective-permute-start | bytes 393224 | tf_op jit(solution)/shard_map/ppermute | solution.py:71
  136.3 5.0 %collective-permute-start.10 = (bf16[4,2,32,256]{3,2,0,1:T(8,128)(2,1)S(1)}, bf16[4,2,32,256]{3,2,0,1:T(8,128)(2,1)S(1)}, u32[]{:S(2)}, u32[]{:S(2)}) collective-permute-start(bf16[4,2,32,256]{3,2,0,1:T(8,128)(2,1)S(1)} %get-tuple-element.56), channel_id=1, source_target_pairs={{0,1},{1,0},{2,3},{3,2},{4,5},{5,4},{6,7},{7,6},{8,9},{9,8},{10,11... | collective-permute-start | bytes 393224 | tf_op jit(solution)/shard_map/ppermute | solution.py:71
  141.3 1.8 copy-start.3
  141.4 1.6 collective-permute-start.13
  147.5 4.5 %copy-start.9 = (s32[32,4]{0,1:T(4,128)S(1)}, s32[32,4]{0,1:T(4,128)}, u32[]{:S(2)}) copy-start(s32[32,4]{0,1:T(4,128)} %param.16) | copy-start | bytes 1540
  147.5 4.6 %copy-start.6 = (f32[32,4,32]{2,1,0:T(4,128)S(1)}, f32[32,4,32]{2,1,0:T(4,128)}, u32[]{:S(2)}) copy-start(f32[32,4,32]{2,1,0:T(4,128)} %param.17) | copy-start | bytes 49156
  147.5 43.1 %all-to-all-start.2 = ((bf16[32,32,768]{2,1,0:T(8,128)(2,1)}), bf16[32,32,768]{2,1,0:T(8,128)(2,1)S(1)}, u32[]{:S(2)}, u32[]{:S(2)}) async-start(bf16[32,32,768]{2,1,0:T(8,128)(2,1)} %get-tuple-element.38), calls=%async_computation.2 | async-start | bytes 3145728 | tf_op jit(solution)/shard_map/all_to_all | solution.py:368
  194.4 3.6 %copy-start.12 = (bf16[8,32,256]{2,1,0:T(8,128)(2,1)S(1)}, bf16[8,32,256]{2,1,0:T(8,128)(2,1)}, u32[]{:S(2)}) copy-start(bf16[8,32,256]{2,1,0:T(8,128)(2,1)} %get-tuple-element.31) | copy-start | bytes 393220
  194.4 5.3 %copy-start.11 = (bf16[8,32,256]{2,1,0:T(8,128)(2,1)S(1)}, bf16[8,32,256]{2,1,0:T(8,128)(2,1)}, u32[]{:S(2)}) copy-start(bf16[8,32,256]{2,1,0:T(8,128)(2,1)} %get-tuple-element.32) | copy-start | bytes 393220
  194.4 7.8 %copy-start.10 = (bf16[8,32,256]{2,1,0:T(8,128)(2,1)S(1)}, bf16[8,32,256]{2,1,0:T(8,128)(2,1)}, u32[]{:S(2)}) copy-start(bf16[8,32,256]{2,1,0:T(8,128)(2,1)} %get-tuple-element.33) | copy-start | bytes 393220
  194.4 49.9 %copy-start.4 = (bf16[8,32,256]{2,1,0:T(8,128)(2,1)S(1)}, bf16[8,32,256]{2,1,0:T(8,128)(2,1)}, u32[]{:S(2)}) copy-start(bf16[8,32,256]{2,1,0:T(8,128)(2,1)} %get-tuple-element.30) | copy-start | bytes 393220
  194.4 96.8 %all-to-all-start.3 = ((bf16[32,32,768]{2,1,0:T(8,128)(2,1)}), bf16[32,32,768]{2,1,0:T(8,128)(2,1)}, u32[]{:S(2)}, u32[]{:S(2)}) async-start(bf16[32,32,768]{2,1,0:T(8,128)(2,1)} %shard_map.98), calls=%async_computation.3 | async-start | bytes 3145728 | tf_op jit(solution)/shard_map/all_to_all | solution.py:368
  198.0 29.0 %collective-permute-start.14 = (bf16[4,2,32,256]{3,2,1,0:T(8,128)(2,1)S(1)}, bf16[4,2,32,256]{3,2,1,0:T(8,128)(2,1)S(1)}, u32[]{:S(2)}, u32[]{:S(2)}) collective-permute-start(bf16[4,2,32,256]{3,2,1,0:T(8,128)(2,1)S(1)} %bitcast.175), channel_id=1, source_target_pairs={{0,2},{1,3},{2,0},{3,1},{4,6},{5,7},{6,4},{7,5},{8,10},{9,11},{10,... | collective-permute-start | bytes 393224 | tf_op jit(solution)/shard_map/ppermute | solution.py:71
  199.7 44.6 %collective-permute-start.15 = (bf16[4,2,32,256]{3,2,1,0:T(8,128)(2,1)S(1)}, bf16[4,2,32,256]{3,2,1,0:T(8,128)(2,1)S(1)}, u32[]{:S(2)}, u32[]{:S(2)}) collective-permute-start(bf16[4,2,32,256]{3,2,1,0:T(8,128)(2,1)S(1)} %bitcast.174), channel_id=1, source_target_pairs={{0,4},{1,5},{2,6},{3,7},{4,0},{5,1},{6,2},{7,3},{8,12},{9,13},{10,... | collective-permute-start | bytes 393224 | tf_op jit(solution)/shard_map/ppermute | solution.py:71
  202.2 42.1 %collective-permute-start.16 = (bf16[4,2,32,256]{3,2,1,0:T(8,128)(2,1)S(1)}, bf16[4,2,32,256]{3,2,1,0:T(8,128)(2,1)S(1)}, u32[]{:S(2)}, u32[]{:S(2)}) collective-permute-start(bf16[4,2,32,256]{3,2,1,0:T(8,128)(2,1)S(1)} %bitcast.173), channel_id=1, source_target_pairs={{0,6},{1,7},{2,4},{3,5},{4,2},{5,3},{6,0},{7,1},{8,14},{9,15},{10,... | collective-permute-start | bytes 393224 | tf_op jit(solution)/shard_map/ppermute | solution.py:71
  244.4 6.9 %collective-permute-start.19 = (bf16[4,2,32,256]{3,2,0,1:T(8,128)(2,1)S(1)}, bf16[4,2,32,256]{3,2,0,1:T(8,128)(2,1)S(1)}, u32[]{:S(2)}, u32[]{:S(2)}) collective-permute-start(bf16[4,2,32,256]{3,2,0,1:T(8,128)(2,1)S(1)} %get-tuple-element.48), channel_id=1, source_target_pairs={{0,17},{1,16},{2,19},{3,18},{4,21},{5,20},{6,23},{7,22},{8,25},{9,... | collective-permute-start | bytes 393224 | tf_op jit(solution)/shard_map/ppermute | solution.py:71
  246.9 5.7 %collective-permute-start.18 = (bf16[4,2,32,256]{3,2,0,1:T(8,128)(2,1)S(1)}, bf16[4,2,32,256]{3,2,0,1:T(8,128)(2,1)S(1)}, u32[]{:S(2)}, u32[]{:S(2)}) collective-permute-start(bf16[4,2,32,256]{3,2,0,1:T(8,128)(2,1)S(1)} %get-tuple-element.49), channel_id=1, source_target_pairs={{0,16},{1,17},{2,18},{3,19},{4,20},{5,21},{6,22},{7,23},{8,24},{9,... | collective-permute-start | bytes 393224 | tf_op jit(solution)/shard_map/ppermute | solution.py:71
  247.4 5.2 %collective-permute-start.17 = (bf16[4,2,32,256]{3,2,0,1:T(8,128)(2,1)S(1)}, bf16[4,2,32,256]{3,2,0,1:T(8,128)(2,1)S(1)}, u32[]{:S(2)}, u32[]{:S(2)}) collective-permute-start(bf16[4,2,32,256]{3,2,0,1:T(8,128)(2,1)S(1)} %get-tuple-element.50), channel_id=1, source_target_pairs={{0,1},{1,0},{2,3},{3,2},{4,5},{5,4},{6,7},{7,6},{8,9},{9,8},{10,11... | collective-permute-start | bytes 393224 | tf_op jit(solution)/shard_map/ppermute | solution.py:71
  252.7 1.6 collective-permute-start.20
  257.3 8.9 %collective-permute-start.21 = (bf16[4,2,32,256]{3,2,1,0:T(8,128)(2,1)}, bf16[4,2,32,256]{3,2,1,0:T(8,128)(2,1)S(1)}, u32[]{:S(2)}, u32[]{:S(2)}) collective-permute-start(bf16[4,2,32,256]{3,2,1,0:T(8,128)(2,1)} %bitcast.183), channel_id=1, source_target_pairs={{0,2},{1,3},{2,0},{3,1},{4,6},{5,7},{6,4},{7,5},{8,10},{9,11},{10,... | collective-permute-start | bytes 393224 | tf_op jit(solution)/shard_map/ppermute | solution.py:71
  260.7 13.1 %collective-permute-start.22 = (bf16[4,2,32,256]{3,2,1,0:T(8,128)(2,1)}, bf16[4,2,32,256]{3,2,1,0:T(8,128)(2,1)S(1)}, u32[]{:S(2)}, u32[]{:S(2)}) collective-permute-start(bf16[4,2,32,256]{3,2,1,0:T(8,128)(2,1)} %bitcast.180), channel_id=1, source_target_pairs={{0,4},{1,5},{2,6},{3,7},{4,0},{5,1},{6,2},{7,3},{8,12},{9,13},{10,... | collective-permute-start | bytes 393224 | tf_op jit(solution)/shard_map/ppermute | solution.py:71
  261.1 12.7 %collective-permute-start.23 = (bf16[4,2,32,256]{3,2,1,0:T(8,128)(2,1)}, bf16[4,2,32,256]{3,2,1,0:T(8,128)(2,1)S(1)}, u32[]{:S(2)}, u32[]{:S(2)}) collective-permute-start(bf16[4,2,32,256]{3,2,1,0:T(8,128)(2,1)} %bitcast.177), channel_id=1, source_target_pairs={{0,6},{1,7},{2,4},{3,5},{4,2},{5,3},{6,0},{7,1},{8,14},{9,15},{10,... | collective-permute-start | bytes 393224 | tf_op jit(solution)/shard_map/ppermute | solution.py:71
  274.8 8.9 %copy-start.7 = (f32[1,1024]{1,0:T(1,128)S(1)}, f32[1,1024]{1,0:T(1,128)}, u32[]{:S(2)}) copy-start(f32[1,1024]{1,0:T(1,128)} %param.11) | copy-start | bytes 12292
  274.8 9.1 %copy-start = (bf16[1,1024,1024]{2,1,0:T(8,128)(2,1)S(1)}, bf16[1,1024,1024]{2,1,0:T(8,128)(2,1)}, u32[]{:S(2)}) copy-start(bf16[1,1024,1024]{2,1,0:T(8,128)(2,1)} %param.9) | copy-start | bytes 6291460
  274.8 6.0 %collective-permute-start.26 = (bf16[4,2,32,256]{3,2,0,1:T(8,128)(2,1)S(1)}, bf16[4,2,32,256]{3,2,0,1:T(8,128)(2,1)S(1)}, u32[]{:S(2)}, u32[]{:S(2)}) collective-permute-start(bf16[4,2,32,256]{3,2,0,1:T(8,128)(2,1)S(1)} %get-tuple-element.42), channel_id=1, source_target_pairs={{0,17},{1,16},{2,19},{3,18},{4,21},{5,20},{6,23},{7,22},{8,25},{9,... | collective-permute-start | bytes 393224 | tf_op jit(solution)/shard_map/ppermute | solution.py:71
  276.6 5.6 %collective-permute-start.25 = (bf16[4,2,32,256]{3,2,0,1:T(8,128)(2,1)S(1)}, bf16[4,2,32,256]{3,2,0,1:T(8,128)(2,1)S(1)}, u32[]{:S(2)}, u32[]{:S(2)}) collective-permute-start(bf16[4,2,32,256]{3,2,0,1:T(8,128)(2,1)S(1)} %get-tuple-element.43), channel_id=1, source_target_pairs={{0,16},{1,17},{2,18},{3,19},{4,20},{5,21},{6,22},{7,23},{8,24},{9,... | collective-permute-start | bytes 393224 | tf_op jit(solution)/shard_map/ppermute | solution.py:71
  277.9 5.0 %collective-permute-start.24 = (bf16[4,2,32,256]{3,2,0,1:T(8,128)(2,1)S(1)}, bf16[4,2,32,256]{3,2,0,1:T(8,128)(2,1)S(1)}, u32[]{:S(2)}, u32[]{:S(2)}) collective-permute-start(bf16[4,2,32,256]{3,2,0,1:T(8,128)(2,1)S(1)} %get-tuple-element.44), channel_id=1, source_target_pairs={{0,1},{1,0},{2,3},{3,2},{4,5},{5,4},{6,7},{7,6},{8,9},{9,8},{10,11... | collective-permute-start | bytes 393224 | tf_op jit(solution)/shard_map/ppermute | solution.py:71
  283.0 8.2 %collective-permute-start.27 = (bf16[4,4,32,256]{3,2,1,0:T(8,128)(2,1)S(1)}, bf16[4,4,32,256]{3,2,1,0:T(8,128)(2,1)S(1)}, u32[]{:S(2)}, u32[]{:S(2)}) collective-permute-start(bf16[4,4,32,256]{3,2,1,0:T(8,128)(2,1)S(1)} %get-tuple-element.40), channel_id=1, source_target_pairs={{0,8},{1,9},{2,10},{3,11},{4,12},{5,13},{6,14},{7,15},{8,0},{9,1},... | collective-permute-start | bytes 786440 | tf_op jit(solution)/shard_map/ppermute | solution.py:71
  283.9 1.6 copy-start.1
